TPU v7x, 128 devices: a whole 4x4x4 slice. The times are simulated.
128 devices in a mesh: cells: 128 (over z, x, y, core).
Axes of the slice: x: 4, y: 4, z: 4, core: 2. Of those that a mesh axis runs over, the one named last changes fastest.
Arguments:
- channels: float32 [256, 41, 64, 128], P('cells'), may hold values from -0.44194174 to 0.44194174, as said below
- precoders_init: float32 [256, 16, 128], P('cells'), may hold values from -1 to 1
- receiver_cells: int32 [256], replicated, may hold values from 0 to 255, as said below
- transmitter_cells: int32 [256], replicated, may hold values from 0 to 255, as said below
- interferers: int32 [256, 40], replicated, may hold values from 0 to 255, as said below
- counts: int32 [256], replicated, may hold values from 24 to 40
Outputs:
- precoders: float32 [256, 16, 128], P('cells')
- mse_weights: float32 [256, 256], P('cells')
Inputs may be any that keep to these rules, and one draw needn't show every extreme that they name: `receiver_cells`: A permutation of the cells; receiver slots s lie on device s // 2. `transmitter_cells`: A permutation of the cells; transmitter slots t lie on device t // 2. `interferers`: each row holds distinct cells, never the cell of its own receiver slot. Over the receiver slots of one device, the links in use (own links included) whose transmitter slot lies on any one device number at most 1, and 1 is reached in every draw. `channels`: own links (m = 0) are drawn stronger than interfering ones.
All inputs are finite; a program needn't handle non-finite values.
Results may differ from a plain program's by a relative error of at most 0.0003.
Values sent between devices are 32-bit elements; how exact they have to be, the bound alone decides.
A program may use at most 64 MiB of HBM per device.

v0:
```python
import jax
import jax.numpy as jnp
from jax import lax
from jax.sharding import PartitionSpec as P

LAYERS = 4


NOISE_POWER = 1.0
STEP_SIZES = (0.3, 0.2, 0.15, 0.1)
HIGHEST = lax.Precision.HIGHEST


def spd_solve(matrix, right_side):
    factor = jnp.linalg.cholesky(matrix)
    middle = lax.linalg.triangular_solve(factor, right_side, left_side=True, lower=True)
    return lax.linalg.triangular_solve(factor, middle, left_side=True, lower=True, transpose_a=True)


def link_tables(receiver_cells, transmitter_cells, interferers, counts):
    inverse = jnp.argsort(transmitter_cells)
    linked = jnp.concatenate([receiver_cells[:, None], interferers], axis=1)
    positions = inverse[linked]
    in_use = jnp.arange(interferers.shape[1] + 1, dtype=jnp.int32)[None, :] <= counts[:, None]
    return (positions, in_use)


def receiver_step(channels, link_precoders, in_use):
    weight_mask = in_use.astype(jnp.float32)
    images = jnp.einsum("klrn,kldn->kldr", channels, link_precoders, precision=HIGHEST)
    masked = images * weight_mask[:, :, None, None]
    receive_size = channels.shape[2]
    stream_count = link_precoders.shape[2]
    covariance = jnp.einsum(
        "kldr,klds->krs", masked, images, precision=HIGHEST
    ) + NOISE_POWER * jnp.eye(receive_size, dtype=jnp.float32)
    direct = images[:, 0]
    filters = spd_solve(covariance, jnp.swapaxes(direct, 1, 2))
    identity = jnp.eye(stream_count, dtype=jnp.float32)
    errors = identity - jnp.einsum("krd,ker->kde", filters, direct, precision=HIGHEST)
    weights = spd_solve(errors, jnp.broadcast_to(identity, errors.shape))
    transposed = (
        jnp.einsum("krd,klrn->kldn", filters, channels, precision=HIGHEST)
        * weight_mask[:, :, None, None]
    )
    return (weights, transposed)


def body(channels, precoders_init, receiver_cells, transmitter_cells, interferers, counts):
    devices = lax.axis_size("cells")
    own_index = lax.axis_index("cells")
    groups = channels.shape[0]
    link_count = channels.shape[1]
    streams = precoders_init.shape[1]
    antennas = precoders_init.shape[2]
    per_device = groups * link_count
    capacity = (per_device + devices - 1) // devices
    slot_total = devices * capacity
    positions, in_use = link_tables(receiver_cells, transmitter_cells, interferers, counts)
    device_of = (positions // groups).reshape(devices, per_device)
    local_of = (positions % groups).reshape(devices, per_device)
    in_service = in_use.reshape(devices, per_device)
    position_index = jnp.arange(per_device, dtype=jnp.int32)
    arriving = in_service & (device_of == own_index)
    ranked = jnp.cumsum(arriving.astype(jnp.int32), axis=1) - 1
    picker = arriving[:, None, :] & (
        ranked[:, None, :] == jnp.arange(capacity, dtype=jnp.int32)[None, :, None]
    )
    slot_used = jnp.any(picker, axis=2).reshape(-1)
    slot_local = jnp.sum(picker * local_of[:, None, :], axis=2).reshape(-1)
    slot_direct = jnp.any(
        picker & (position_index % link_count == 0)[None, None, :], axis=2
    ).reshape(-1)
    mine_device = device_of[own_index]
    mine_service = in_service[own_index]
    mine_positions = positions.reshape(devices, per_device)[own_index]
    earlier = (
        mine_service[None, :]
        & (mine_device[None, :] == mine_device[:, None])
        & (position_index[None, :] < position_index[:, None])
    )
    mine_rank = jnp.sum(earlier.astype(jnp.int32), axis=1)
    mine_index = jnp.where(mine_service, mine_device * capacity + mine_rank, 0)
    back_pick = mine_service[None, :] & (
        mine_index[None, :] == jnp.arange(slot_total, dtype=jnp.int32)[:, None]
    )
    back_used = jnp.any(back_pick, axis=1).astype(jnp.float32)
    back_position = jnp.sum(back_pick * position_index[None, :], axis=1)
    my_in_use = in_use.reshape(devices, groups, link_count)[own_index]
    target_mask = (
        (slot_local[None, :] == jnp.arange(groups, dtype=jnp.int32)[:, None]) & slot_used[None, :]
    ).astype(jnp.float32)
    direct_mask = target_mask * slot_direct.astype(jnp.float32)[None, :]
    precoders = precoders_init
    weights = jnp.zeros((groups, streams, streams), jnp.float32)
    for layer_index in range(LAYERS):
        everything = lax.all_gather(precoders, "cells", axis=0, tiled=True)
        link_precoders = everything[mine_positions]
        weights, transposed = receiver_step(
            channels, link_precoders.reshape(groups, link_count, streams, antennas), my_in_use
        )
        flat_filters = transposed.reshape(per_device, streams, antennas)
        outgoing_filters = (flat_filters[back_position] * back_used[:, None, None]).reshape(
            devices, capacity, streams, antennas
        )
        link_weights = (
            weights.reshape(groups, streams * streams)[back_position // link_count]
            * back_used[:, None]
        )
        arrived, arrived_weights = (
            lax.all_to_all(outgoing_filters, "cells", split_axis=0, concat_axis=0, tiled=True),
            lax.all_to_all(
                link_weights.reshape(devices, capacity, streams * streams),
                "cells",
                split_axis=0,
                concat_axis=0,
                tiled=True,
            ),
        )
        arrived_weights = arrived_weights.reshape(slot_total, streams, streams)
        arrived = arrived.reshape(slot_total, streams, antennas)
        weighted = jnp.einsum("sed,sen->sdn", arrived_weights, arrived, precision=HIGHEST)
        selected = target_mask[:, :, None, None] * arrived[None]
        system = jnp.einsum("gsdn,sdm->gnm", selected, weighted, precision=HIGHEST)
        system = system + STEP_SIZES[layer_index] * jnp.eye(antennas, dtype=jnp.float32)
        right_side = jnp.einsum("gs,sdn->gdn", direct_mask, weighted, precision=HIGHEST)
        precoders = jnp.swapaxes(spd_solve(system, jnp.swapaxes(right_side, 1, 2)), 1, 2)
    return (precoders, weights.reshape(groups, streams * streams))


def solution(mesh):
    return jax.shard_map(
        body,
        mesh=mesh,
        in_specs=(P("cells", None, None, None), P("cells", None, None), P(), P(), P(), P()),
        out_specs=(P("cells", None, None), P("cells", None)),
        check_vma=False,
    )
```

profile of v0, /device:TPU:1, one launch (start us, length us, event | category | flops | bytes accessed | tf_op | source)
XLA Modules:
  0.0 852.8 jit_solution(2282363171503754856)
XLA Ops:
  13.8 61.3 %gather_fusion = s32[10496]{0:T(1024)S(1)} fusion(s32[256]{0:T(256)S(1)} %get-tuple-element.6, s32[11264]{0:T(1024)S(1)} %pad_clamp_fusion), kind=kCustom, calls=%fused_computation | custom fusion | bytes 125952 | tf_op jit(solution)/shard_map/gather | solution.py:23
  83.4 5.4 broadcast_multiply_fusion.3
  92.7 12.5 %custom-call.54 = f32[2,64,64]{2,1,0:T(8,128)S(1)} custom-call(f32[2,64,64]{2,1,0:T(8,128)} %fusion.99), custom_call_target="Cholesky" | custom-call | tf_op jit(solution)/shard_map/jit(cholesky)/cholesky | solution.py:15
  106.0 10.6 %custom-call.56 = f32[2,1,64,64]{2,3,1,0:T(8,128)S(1)} custom-call(f32[2,1,64,64]{3,2,1,0:T(8,128)} %select_bitcast_fusion.7), custom_call_target="InvertDiagBlocksLowerTriangular" | custom-call | tf_op jit(solution)/shard_map/triangular_solve/custom-call.4 | solution.py:17
  130.1 12.0 %all-to-all-start.1 = ((f32[128,1,256]{2,1,0:T(1,128)}), f32[128,1,256]{2,1,0:T(1,128)}, u32[]{:S(2)}, u32[]{:S(2)}) async-start(f32[128,1,256]{2,1,0:T(1,128)} %copy.284), calls=%async_computation.1 | async-start | bytes 262144 | tf_op jit(solution)/shard_map/all_to_all | solution.py:112
  160.2 15.4 %all-to-all-done = f32[128,1,16,128]{3,2,1,0:T(8,128)} async-done(((f32[128,1,16,128]{3,2,1,0:T(8,128)}), f32[128,1,16,128]{3,2,1,0:T(8,128)}, u32[]{:S(2)}, u32[]{:S(2)}) %all-to-all-start) | async-done | bytes 1048608 | tf_op jit(solution)/shard_map/all_to_all | solution.py:111
  184.3 23.5 %custom-call.60 = f32[2,128,128]{2,1,0:T(8,128)S(1)} custom-call(f32[2,128,128]{2,1,0:T(8,128)S(1)} %fusion.79), custom_call_target="Cholesky" | custom-call | tf_op jit(solution)/shard_map/jit(cholesky)/cholesky | solution.py:15
  208.0 19.7 %custom-call.62 = f32[2,1,128,128]{2,3,1,0:T(8,128)S(1)} custom-call(f32[2,1,128,128]{3,2,1,0:T(8,128)S(1)} %select_bitcast_fusion.3), custom_call_target="InvertDiagBlocksLowerTriangular" | custom-call | tf_op jit(solution)/shard_map/triangular_solve/custom-call.8 | solution.py:17
  230.9 62.4 %all-gather.7.cloned.1.call-done = f32[256,16,128]{2,1,0:T(8,128)} async-done(((f32[2,16,128]{2,1,0:T(8,128)}), f32[256,16,128]{2,1,0:T(8,128)}) %all-gather.7.cloned.1.call-update) | async-done | bytes 2097168 | tf_op jit(solution)/shard_map/all_gather | solution.py:97
  296.5 5.4 broadcast_multiply_fusion.2
  305.9 12.6 %custom-call.63 = f32[2,64,64]{2,1,0:T(8,128)S(1)} custom-call(f32[2,64,64]{2,1,0:T(8,128)} %fusion.94), custom_call_target="Cholesky" | custom-call | tf_op jit(solution)/shard_map/jit(cholesky)/cholesky | solution.py:15
  319.3 10.6 %custom-call.65 = f32[2,1,64,64]{2,3,1,0:T(8,128)S(1)} custom-call(f32[2,1,64,64]{3,2,1,0:T(8,128)} %select_bitcast_fusion.6), custom_call_target="InvertDiagBlocksLowerTriangular" | custom-call | tf_op jit(solution)/shard_map/triangular_solve/custom-call.4 | solution.py:17
  342.7 5.8 all-to-all-start.3
  352.8 5.5 all-to-all-done.3
  366.1 16.0 %all-to-all-done.2 = f32[128,1,16,128]{3,2,1,0:T(8,128)} async-done(((f32[128,1,16,128]{3,2,1,0:T(8,128)}), f32[128,1,16,128]{3,2,1,0:T(8,128)}, u32[]{:S(2)}, u32[]{:S(2)}) %all-to-all-start.2) | async-done | bytes 1048608 | tf_op jit(solution)/shard_map/all_to_all | solution.py:111
  393.0 23.7 %custom-call.69 = f32[2,128,128]{2,1,0:T(8,128)S(1)} custom-call(f32[2,128,128]{2,1,0:T(8,128)S(1)} %fusion.75), custom_call_target="Cholesky" | custom-call | tf_op jit(solution)/shard_map/jit(cholesky)/cholesky | solution.py:15
  416.9 19.7 %custom-call.71 = f32[2,1,128,128]{2,3,1,0:T(8,128)S(1)} custom-call(f32[2,1,128,128]{3,2,1,0:T(8,128)S(1)} %select_bitcast_fusion.2), custom_call_target="InvertDiagBlocksLowerTriangular" | custom-call | tf_op jit(solution)/shard_map/triangular_solve/custom-call.8 | solution.py:17
  437.8 62.4 %all-gather.9.cloned.1.call-done = f32[256,16,128]{2,1,0:T(8,128)} async-done(((f32[2,16,128]{2,1,0:T(8,128)}), f32[256,16,128]{2,1,0:T(8,128)}) %all-gather.9.cloned.1.call-update) | async-done | bytes 2097168 | tf_op jit(solution)/shard_map/all_gather | solution.py:97
  512.7 12.9 %custom-call.72 = f32[2,64,64]{2,1,0:T(8,128)S(1)} custom-call(f32[2,64,64]{2,1,0:T(8,128)} %fusion.89), custom_call_target="Cholesky" | custom-call | tf_op jit(solution)/shard_map/jit(cholesky)/cholesky | solution.py:15
  526.4 10.6 %custom-call.74 = f32[2,1,64,64]{2,3,1,0:T(8,128)S(1)} custom-call(f32[2,1,64,64]{3,2,1,0:T(8,128)} %select_bitcast_fusion.5), custom_call_target="InvertDiagBlocksLowerTriangular" | custom-call | tf_op jit(solution)/shard_map/triangular_solve/custom-call.4 | solution.py:17
  548.5 5.8 all-to-all-start.5
  558.5 5.5 all-to-all-done.5
  571.8 16.0 %all-to-all-done.4 = f32[128,1,16,128]{3,2,1,0:T(8,128)} async-done(((f32[128,1,16,128]{3,2,1,0:T(8,128)}), f32[128,1,16,128]{3,2,1,0:T(8,128)}, u32[]{:S(2)}, u32[]{:S(2)}) %all-to-all-start.4) | async-done | bytes 1048608 | tf_op jit(solution)/shard_map/all_to_all | solution.py:111
  598.7 23.6 %custom-call.78 = f32[2,128,128]{2,1,0:T(8,128)S(1)} custom-call(f32[2,128,128]{2,1,0:T(8,128)S(1)} %fusion.71), custom_call_target="Cholesky" | custom-call | tf_op jit(solution)/shard_map/jit(cholesky)/cholesky | solution.py:15
  622.6 19.7 %custom-call.80 = f32[2,1,128,128]{2,3,1,0:T(8,128)S(1)} custom-call(f32[2,1,128,128]{3,2,1,0:T(8,128)S(1)} %select_bitcast_fusion.1), custom_call_target="InvertDiagBlocksLowerTriangular" | custom-call | tf_op jit(solution)/shard_map/triangular_solve/custom-call.8 | solution.py:17
  643.5 62.4 %all-gather.11.cloned.1.call-done = f32[256,16,128]{2,1,0:T(8,128)} async-done(((f32[2,16,128]{2,1,0:T(8,128)}), f32[256,16,128]{2,1,0:T(8,128)}) %all-gather.11.cloned.1.call-update) | async-done | bytes 2097168 | tf_op jit(solution)/shard_map/all_gather | solution.py:97
  716.9 12.5 %custom-call.81 = f32[2,64,64]{2,1,0:T(8,128)S(1)} custom-call(f32[2,64,64]{2,1,0:T(8,128)} %fusion.84), custom_call_target="Cholesky" | custom-call | tf_op jit(solution)/shard_map/jit(cholesky)/cholesky | solution.py:15
  730.3 9.8 %custom-call.83 = f32[2,1,64,64]{2,3,1,0:T(8,128)S(1)} custom-call(f32[2,1,64,64]{3,2,1,0:T(8,128)S(1)} %select_bitcast_fusion.4), custom_call_target="InvertDiagBlocksLowerTriangular" | custom-call | tf_op jit(solution)/shard_map/triangular_solve/custom-call.4 | solution.py:17
  761.0 5.6 all-to-all-done.7
  773.6 16.9 %all-to-all-done.6 = f32[128,1,16,128]{3,2,1,0:T(8,128)} async-done(((f32[128,1,16,128]{3,2,1,0:T(8,128)}), f32[128,1,16,128]{3,2,1,0:T(8,128)}, u32[]{:S(2)}, u32[]{:S(2)}) %all-to-all-start.6) | async-done | bytes 1048608 | tf_op jit(solution)/shard_map/all_to_all | solution.py:111
  801.3 23.5 %custom-call.87 = f32[2,128,128]{2,1,0:T(8,128)S(1)} custom-call(f32[2,128,128]{2,1,0:T(8,128)S(1)} %fusion.67), custom_call_target="Cholesky" | custom-call | tf_op jit(solution)/shard_map/jit(cholesky)/cholesky | solution.py:15
  825.0 19.7 %custom-call.89 = f32[2,1,128,128]{2,3,1,0:T(8,128)S(1)} custom-call(f32[2,1,128,128]{3,2,1,0:T(8,128)S(1)} %select_bitcast_fusion), custom_call_target="InvertDiagBlocksLowerTriangular" | custom-call | tf_op jit(solution)/shard_map/triangular_solve/custom-call.8 | solution.py:17
  (298 shorter events, 208.9 us)
Async XLA Ops:
  7.2 76.2 %copy-start = (f32[2,41,64,128]{3,2,1,0:T(8,128)S(1)}, f32[2,41,64,128]{3,2,1,0:T(8,128)}, u32[]{:S(2)}) copy-start(f32[2,41,64,128]{3,2,1,0:T(8,128)} %param.21) | copy-start | bytes 8060932
  7.2 73.1 %all-gather.5.cloned.1.call-start = ((), (), s32[]{:S(2)}) async-start(), calls=%async_computation.8 | async-start | bytes 2113536 | tf_op jit(solution)/shard_map/all_gather | solution.py:97
  78.9 26.2 %copy-start.10 = (pred[64,64]{1,0:T(8,128)(4,1)}, pred[64,64]{1,0:T(8,128)(4,1)S(1)}, u32[]{:S(2)}) copy-start(pred[64,64]{1,0:T(8,128)(4,1)S(1)} %iota_compare_fusion.6) | copy-start | bytes 12292
  79.8 37.2 %copy-start.13 = (f32[2,41]{1,0:T(2,128)}, f32[2,41]{1,0:T(2,128)S(1)}, u32[]{:S(2)}) copy-start(f32[2,41]{1,0:T(2,128)S(1)} %fusion.166) | copy-start | bytes 988
  88.7 28.0 %copy-start.7 = (f32[2,41,16,64]{3,2,1,0:T(8,128)}, f32[2,41,16,64]{3,2,1,0:T(8,128)S(1)}, u32[]{:S(2)}) copy-start(f32[2,41,16,64]{3,2,1,0:T(8,128)S(1)} %get-tuple-element.24) | copy-start | bytes 1007620
  130.1 21.8 %all-to-all-start.1 = ((f32[128,1,256]{2,1,0:T(1,128)}), f32[128,1,256]{2,1,0:T(1,128)}, u32[]{:S(2)}, u32[]{:S(2)}) async-start(f32[128,1,256]{2,1,0:T(1,128)} %copy.284), calls=%async_computation.1 | async-start | bytes 262144 | tf_op jit(solution)/shard_map/all_to_all | solution.py:112
  151.9 23.8 %all-to-all-start = ((f32[128,1,16,128]{3,2,1,0:T(8,128)}), f32[128,1,16,128]{3,2,1,0:T(8,128)}, u32[]{:S(2)}, u32[]{:S(2)}) async-start(f32[128,1,16,128]{3,2,1,0:T(8,128)} %bitcast_multiply_fusion.3), calls=%async_computation | async-start | bytes 2097152 | tf_op jit(solution)/shard_map/all_to_all | solution.py:111
  157.1 136.3 %all-gather.7.cloned.1.call-start = ((), (), s32[]{:S(2)}) async-start(), calls=%async_computation.9 | async-start | bytes 2113536 | tf_op jit(solution)/shard_map/all_gather | solution.py:97
  157.7 69.9 %copy-start.31 = (f32[128]{0:T(128)}, f32[128]{0:T(128)S(1)}, u32[]{:S(2)}) copy-start(f32[128]{0:T(128)S(1)} %convert_element_type.98) | copy-start | bytes 1540
  157.8 23.2 %copy-start.22 = (f32[2,128]{1,0:T(2,128)}, f32[2,128]{1,0:T(2,128)S(1)}, u32[]{:S(2)}) copy-start(f32[2,128]{1,0:T(2,128)S(1)} %get-tuple-element.12) | copy-start | bytes 3076
  157.8 69.8 %copy-start.26 = (pred[2,128]{1,0:T(4,128)(4,1)}, pred[2,128]{1,0:T(4,128)(4,1)S(1)}, u32[]{:S(2)}) copy-start(pred[2,128]{1,0:T(4,128)(4,1)S(1)} %get-tuple-element.14) | copy-start | bytes 772
  182.0 114.5 %copy-start.14 = (f32[2,41]{1,0:T(2,128)S(1)}, f32[2,41]{1,0:T(2,128)}, u32[]{:S(2)}) copy-start(f32[2,41]{1,0:T(2,128)} %copy-done.13) | copy-start | bytes 988
  342.7 15.6 %all-to-all-start.3 = ((f32[128,1,256]{2,1,0:T(1,128)}), f32[128,1,256]{2,1,0:T(1,128)}, u32[]{:S(2)}, u32[]{:S(2)}) async-start(f32[128,1,256]{2,1,0:T(1,128)} %copy.308), calls=%async_computation.3 | async-start | bytes 262144 | tf_op jit(solution)/shard_map/all_to_all | solution.py:112
  358.3 23.8 %all-to-all-start.2 = ((f32[128,1,16,128]{3,2,1,0:T(8,128)}), f32[128,1,16,128]{3,2,1,0:T(8,128)}, u32[]{:S(2)}, u32[]{:S(2)}) async-start(f32[128,1,16,128]{3,2,1,0:T(8,128)} %bitcast_multiply_fusion.2), calls=%async_computation.2 | async-start | bytes 2097152 | tf_op jit(solution)/shard_map/all_to_all | solution.py:111
  363.5 22.3 %copy-start.27 = (pred[2,128]{1,0:T(4,128)(4,1)S(1)}, pred[2,128]{1,0:T(4,128)(4,1)}, u32[]{:S(2)}) copy-start(pred[2,128]{1,0:T(4,128)(4,1)} %copy-done.26) | copy-start | bytes 772
  363.5 22.2 %copy-start.32 = (f32[128]{0:T(128)S(1)}, f32[128]{0:T(128)}, u32[]{:S(2)}) copy-start(f32[128]{0:T(128)} %copy-done.31) | copy-start | bytes 1540
  363.5 136.6 %all-gather.9.cloned.1.call-start = ((), (), s32[]{:S(2)}) async-start(), calls=%async_computation.10 | async-start | bytes 2113536 | tf_op jit(solution)/shard_map/all_gather | solution.py:97
  366.0 23.2 %copy-start.23 = (f32[2,128]{1,0:T(2,128)S(1)}, f32[2,128]{1,0:T(2,128)}, u32[]{:S(2)}) copy-start(f32[2,128]{1,0:T(2,128)} %copy-done.22) | copy-start | bytes 3076
  508.7 33.3 %copy-start.17 = (pred[16,16]{1,0:T(8,128)(4,1)S(1)}, pred[16,16]{1,0:T(8,128)(4,1)}, u32[]{:S(2)}) copy-start(pred[16,16]{1,0:T(8,128)(4,1)} %iota_compare_fusion.9) | copy-start | bytes 772
  508.7 33.4 %copy-start.15 = (pred[16,16]{1,0:T(8,128)(4,1)S(1)}, pred[16,16]{1,0:T(8,128)(4,1)}, u32[]{:S(2)}) copy-start(pred[16,16]{1,0:T(8,128)(4,1)} %iota_compare_fusion.8) | copy-start | bytes 772
  548.5 15.6 %all-to-all-start.5 = ((f32[128,1,256]{2,1,0:T(1,128)}), f32[128,1,256]{2,1,0:T(1,128)}, u32[]{:S(2)}, u32[]{:S(2)}) async-start(f32[128,1,256]{2,1,0:T(1,128)} %copy.332), calls=%async_computation.5 | async-start | bytes 262144 | tf_op jit(solution)/shard_map/all_to_all | solution.py:112
  564.1 23.8 %all-to-all-start.4 = ((f32[128,1,16,128]{3,2,1,0:T(8,128)}), f32[128,1,16,128]{3,2,1,0:T(8,128)}, u32[]{:S(2)}, u32[]{:S(2)}) async-start(f32[128,1,16,128]{3,2,1,0:T(8,128)} %bitcast_multiply_fusion.1), calls=%async_computation.4 | async-start | bytes 2097152 | tf_op jit(solution)/shard_map/all_to_all | solution.py:111
  569.2 22.3 %copy-start.28 = (pred[2,128]{1,0:T(4,128)(4,1)S(1)}, pred[2,128]{1,0:T(4,128)(4,1)}, u32[]{:S(2)}) copy-start(pred[2,128]{1,0:T(4,128)(4,1)} %copy-done.26) | copy-start | bytes 772
  569.3 22.2 %copy-start.33 = (f32[128]{0:T(128)S(1)}, f32[128]{0:T(128)}, u32[]{:S(2)}) copy-start(f32[128]{0:T(128)} %copy-done.31) | copy-start | bytes 1540
  569.3 136.6 %all-gather.11.cloned.1.call-start = ((), (), s32[]{:S(2)}) async-start(), calls=%async_computation.11 | async-start | bytes 2113536 | tf_op jit(solution)/shard_map/all_gather | solution.py:97
  571.8 23.2 %copy-start.24 = (f32[2,128]{1,0:T(2,128)S(1)}, f32[2,128]{1,0:T(2,128)}, u32[]{:S(2)}) copy-start(f32[2,128]{1,0:T(2,128)} %copy-done.22) | copy-start | bytes 3076
  716.2 29.6 %copy-start.18 = (pred[16,16]{1,0:T(8,128)(4,1)S(1)}, pred[16,16]{1,0:T(8,128)(4,1)}, u32[]{:S(2)}) copy-start(pred[16,16]{1,0:T(8,128)(4,1)} %iota_compare_fusion.9) | copy-start | bytes 772
  716.2 29.8 %copy-start.16 = (pred[16,16]{1,0:T(8,128)(4,1)S(1)}, pred[16,16]{1,0:T(8,128)(4,1)}, u32[]{:S(2)}) copy-start(pred[16,16]{1,0:T(8,128)(4,1)} %iota_compare_fusion.8) | copy-start | bytes 772
  751.3 15.3 %all-to-all-start.7 = ((f32[128,1,256]{2,1,0:T(1,128)}), f32[128,1,256]{2,1,0:T(1,128)S(1)}, u32[]{:S(2)}, u32[]{:S(2)}) async-start(f32[128,1,256]{2,1,0:T(1,128)} %copy.356), calls=%async_computation.7 | async-start | bytes 262144 | tf_op jit(solution)/shard_map/all_to_all | solution.py:112
  766.7 23.8 %all-to-all-start.6 = ((f32[128,1,16,128]{3,2,1,0:T(8,128)}), f32[128,1,16,128]{3,2,1,0:T(8,128)}, u32[]{:S(2)}, u32[]{:S(2)}) async-start(f32[128,1,16,128]{3,2,1,0:T(8,128)} %bitcast_multiply_fusion), calls=%async_computation.6 | async-start | bytes 2097152 | tf_op jit(solution)/shard_map/all_to_all | solution.py:111
  772.0 22.1 %copy-start.29 = (pred[2,128]{1,0:T(4,128)(4,1)S(1)}, pred[2,128]{1,0:T(4,128)(4,1)}, u32[]{:S(2)}) copy-start(pred[2,128]{1,0:T(4,128)(4,1)} %copy-done.26) | copy-start | bytes 772
  773.6 24.1 %copy-start.25 = (f32[2,128]{1,0:T(2,128)S(1)}, f32[2,128]{1,0:T(2,128)}, u32[]{:S(2)}) copy-start(f32[2,128]{1,0:T(2,128)} %copy-done.22) | copy-start | bytes 3076
  (17 other events, 182.5 us)
Sparse Core Ops, SparseCore 0:
  11.1 69.1 all-gather.4
  231.1 62.2 all-gather.6
  437.9 62.2 all-gather.8
  643.6 62.2 all-gather.10
where the time goes:
time: 864 us; the launch traced here: 853 us
  other arithmetic  322 us (37%)
  waiting for transfers between devices  275 us (32%)
  local copies, waits for them, and re-layouts  119 us (14%)
  matrix products  72.2 us (8%)
  starting transfers between devices  49.9 us (6%)
  between operations  15.1 us (2%)
    all_gather x4, waiting for transfers between devices, body(): everything = lax.all_gather(precoders, 'cells', axis=0, tiled=True)  188 us
    another operation x39, other arithmetic, spd_solve(): factor = jnp.linalg.cholesky(matrix)  161 us
    another operation x27, other arithmetic, spd_solve(): lax.linalg.triangular_solve(factor, middle, left_side=True, lower=True, t...  135 us
    all_to_all x4, waiting for transfers between devices, body(): lax.all_to_all(outgoing_filters, 'cells', split_axis=0, concat_axis=0, ti...  64.3 us
    gather x5, local copies, waits for them, and re-layouts, link_tables(): positions = inverse[linked]  61.7 us
    all_to_all x4, starting transfers between devices, body(): lax.all_to_all(link_weights.reshape(devices, capacity, streams * streams)...  28.9 us
    all_to_all x4, waiting for transfers between devices, body(): lax.all_to_all(link_weights.reshape(devices, capacity, streams * streams)...  22 us
    dot_general x4, matrix products, receiver_step(): jnp.einsum('klrn,kldn->kldr', channels, link_precoders, precision=HIGHEST)  21.5 us
  transfers between devices with their start and end apart: 12, of which 12 were waited for; matrix products, arithmetic and copies ran while one was open for 12% of the time, Pallas kernels for 0%

commit v1 on v0

v1 whole, which is shorter than its diff:
```python
import functools

import jax
import jax.numpy as jnp
from jax import lax
from jax.experimental import pallas as pl
from jax.experimental.pallas import tpu as pltpu
from jax.sharding import PartitionSpec as P

LAYERS = 4
STEP_SIZES = (0.3, 0.2, 0.15, 0.1)
HIGHEST = lax.Precision.HIGHEST
MESH = pl.DeviceIdType.MESH
F32, BF16 = jnp.float32, jnp.bfloat16
DEV = 128
GROUP = 16
GROUPS = DEV // GROUP
BLOCK = 8
NN = (((1,), (0,)), ((), ()))
NT = (((1,), (1,)), ((), ()))
TN = (((0,), (0,)), ((), ()))


def split(x):
    high = x.astype(BF16)
    return high, (x - high.astype(F32)).astype(BF16)


def mm(a, b, dims):
    return lax.dot_general(a, b, dims, preferred_element_type=F32)


def mm_exact(a, b, dims):
    return lax.dot_general(a, b, dims, precision=HIGHEST, preferred_element_type=F32)


def lanes():
    return lax.broadcasted_iota(jnp.int32, (8, 128), 1)


def pick_row(v, row):
    return jnp.broadcast_to(v[row : row + 1, :], (8, 128))


def pick_lane(v, k):
    return jnp.where(
        lanes() < 64,
        jnp.broadcast_to(v[:, k : k + 1], (8, 128)),
        jnp.broadcast_to(v[:, 64 + k : 65 + k], (8, 128)),
    )


def rows_of(x):
    return [x[8 * i : 8 * i + 8, :] for i in range(x.shape[0] // 8)]


def right_divide(rows):
    rows = list(rows)
    count = len(rows)
    spot = lanes() % 64
    for first in range(0, 64, BLOCK):
        top = first // 8
        columns = [{i: pick_lane(rows[i], first + j) for i in range(top, count)} for j in range(BLOCK)]
        pivots = [pick_row(rows[top], j) for j in range(BLOCK)]
        scaled = []
        for j in range(BLOCK):
            inverse = 1.0 / pick_row(columns[j][top], j)
            row = (pivots[j] - (spot == first + j).astype(F32)) * inverse
            scaled.append(row)
            for later in range(j + 1, BLOCK):
                factor = pick_row(columns[later][top], j) * inverse
                for i in range(top, count):
                    columns[later][i] = columns[later][i] - columns[j][i] * factor
                pivots[later] = pivots[later] - pick_row(columns[j][top], later) * row
        for i in range(top, count):
            total = rows[i]
            for j in range(BLOCK):
                total = total - columns[j][i] * scaled[j]
            rows[i] = total
    return rows[8:]


def lower_divide(w, v):
    ws, vs = rows_of(w), rows_of(v)
    line = lax.broadcasted_iota(jnp.int32, (8, 128), 0)
    diagonal = [jnp.ones((8, 128), F32), jnp.ones((8, 128), F32)]
    for k in range(16):
        top, at = divmod(k, 8)
        columns = {i: pick_lane(ws[i], k) for i in range(top, 2)}
        pivot = pick_row(columns[top], at)
        inverse = 1.0 / pivot
        wrow, vrow = pick_row(ws[top], at) * inverse, pick_row(vs[top], at) * inverse
        diagonal[top] = jnp.where(line == at, pivot, diagonal[top])
        for i in range(top, 2):
            column = jnp.where(line > at, columns[i], 0.0) if i == top else columns[i]
            ws[i] = ws[i] - column * wrow
            vs[i] = vs[i] - column * vrow
    out_l, out_v = [], []
    for i in range(2):
        scale = 1.0 / jnp.sqrt(diagonal[i])
        keep = (lanes() % 64 >= line + 8 * i) & (lanes() % 64 < 16)
        out_l.append(jnp.where(keep, ws[i] * scale, 0.0))
        out_v.append(vs[i] * scale)
    return out_l, jnp.concatenate(out_v, axis=0)


def kernel(
    tab, channels, first_precoders, precoders_out, weights_out,
    raw, links, current, psend, parr, gbuf, fsend, farr, lsend, larr, pair, acc1, acc2,
    raw_sem, psend_sem, precv, fsend_sem, frecv, lsend_sem, lrecv,
):
    me = lax.axis_index("cells")
    mz, mx, my, mc = me // 32, (me // 8) % 4, (me // 2) % 4, me % 2

    def target(i):
        dz, dx, dy, dc = i // 32, (i // 8) % 4, (i // 2) % 4, i % 2
        return (((mz + dz) % 4 * 4 + (mx + dx) % 4) * 4 + (my + dy) % 4) * 2 + (mc + dc) % 2

    def source(i):
        dz, dx, dy, dc = i // 32, (i // 8) % 4, (i // 2) % 4, i % 2
        return (((mz + 4 - dz) % 4 * 4 + (mx + 4 - dx) % 4) * 4 + (my + 4 - dy) % 4) * 2 + (mc + 2 - dc) % 2

    def step_from(d):
        z, x, y, c = d // 32, (d // 8) % 4, (d // 2) % 4, d % 2
        return (((mz + 4 - z) % 4 * 4 + (mx + 4 - x) % 4) * 4 + (my + 4 - y) % 4) * 2 + (mc + 2 - c) % 2

    def copy(src, dst, i, send, recv):
        return pltpu.make_async_remote_copy(
            src_ref=src, dst_ref=dst, send_sem=send, recv_sem=recv,
            device_id=(target(i),), device_id_type=MESH,
        )

    def wait_group(buf, g, send, recv, first):
        @pl.when(g == 0)
        def _():
            part = buf.at[pl.ds(1, GROUP - 1)]
            copy(part, part, 1, send, recv.at[0]).wait_recv()

        @pl.when(g > 0)
        def _():
            part = buf.at[pl.ds(g * GROUP, GROUP)]
            copy(part, part, 1, send, recv.at[g]).wait_recv()

    fetch = pltpu.make_async_copy(channels, raw, raw_sem)
    fetch.start()
    barrier = pltpu.get_barrier_semaphore()

    def greet(i, carry):
        pl.semaphore_signal(barrier, inc=1, device_id=(target(i),), device_id_type=MESH)
        return carry

    lax.fori_loop(1, DEV, greet, 0)
    current[...] = first_precoders[...]
    half = lax.broadcasted_iota(jnp.int32, (16, 128), 1) < 64
    left = lax.broadcasted_iota(jnp.int32, (64, 128), 1) < 64
    pl.semaphore_wait(barrier, DEV - 1)
    fetch.wait()

    def prepare(i, carry):
        high, low = split(raw[i])
        links[i, 0:64, :] = high
        links[i, 64:128, :] = low
        return carry

    def layer(index, carry):
        def select(i, carry):
            psend[i] = current[tab[4, target(i)]]
            return carry

        lax.fori_loop(0, DEV, select, 0, unroll=8)
        parr[0] = psend[0]

        def send_precoder(i, carry):
            copy(psend.at[i], parr.at[i], i, psend_sem, precv.at[i // GROUP]).start()
            return carry

        lax.fori_loop(1, DEV, send_precoder, 0)

        @pl.when(index == 0)
        def _():
            lax.fori_loop(0, 82, prepare, 0)

        acc1[...] = jnp.zeros((128, 256), F32)
        acc2[...] = jnp.zeros((128, 256), F32)

        def images(g, carry):
            wait_group(parr, g, psend_sem, precv, 1)
            highs, lows = [], []
            for j in range(GROUP):
                i = g * GROUP + j
                d = source(i)
                high, low = split(parr[i])
                product = mm(jnp.concatenate([high, low], axis=0), links[tab[0, d]], NT)
                total = product[0:16] + product[16:32]
                total = total + pltpu.roll(total, 64, 1)
                gbuf[i] = total
                masked = total * jnp.where(half, tab[1, d].astype(F32), tab[2, d].astype(F32))
                high, low = split(masked)
                highs.append(high)
                lows.append(low)
            high, low = jnp.concatenate(highs, axis=0), jnp.concatenate(lows, axis=0)
            acc1[:, 0:128] += mm(high, high, TN)
            acc2[:, 0:128] += mm(high, low, TN)
            return carry

        lax.fori_loop(0, GROUPS, images, 0)
        cross = acc2[:, 0:128]
        full = acc1[:, 0:128] + cross + cross.T
        line = lax.broadcasted_iota(jnp.int32, (64, 128), 0)
        spot = lax.broadcasted_iota(jnp.int32, (64, 128), 1) % 64
        covariance = jnp.where(left, full[0:64], full[64:128]) + (line == spot).astype(F32)
        direct = jnp.where(half, gbuf[step_from(tab[5, 0])], gbuf[step_from(tab[5, 1])])
        v = jnp.concatenate(right_divide(rows_of(covariance) + rows_of(direct))[0:2], axis=0)
        blank = jnp.zeros((48, 128), F32)
        apart = jnp.concatenate(
            [jnp.where(half, direct, 0.0), blank, jnp.where(half, 0.0, direct), blank], axis=0
        )
        short = lax.broadcasted_iota(jnp.int32, (16, 128), 0)
        w = mm_exact(v, apart, NT)
        w = w + (lax.broadcasted_iota(jnp.int32, (16, 128), 1) % 64 == short).astype(F32)
        weights_out[...] = w
        lower, filters = lower_divide(w, v)
        for s in range(2):
            mine = jnp.where(half, filters, 0.0) if s == 0 else jnp.where(half, 0.0, filters)
            mine = mine + pltpu.roll(mine, 64, 1)
            high, low = split(mine)
            pair[s] = jnp.concatenate([high, low], axis=0)
        packed = lower[0] + pltpu.roll(lower[1], 16, 1)

        def filter_group(g, carry):
            for j in range(GROUP):
                i = g * GROUP + j
                at = tab[0, target(i)]
                product = mm(pair[at // 41], links[at], NN)
                fsend[i] = product[0:16] + product[16:32]

            def send_filter(i, carry):
                copy(fsend.at[i], farr.at[i], i, fsend_sem, frecv.at[i // GROUP]).start()
                return carry

            lax.fori_loop(jnp.where(g == 0, 1, g * GROUP), (g + 1) * GROUP, send_filter, 0)
            return carry

        lax.fori_loop(0, GROUPS, filter_group, 0)
        farr[0] = fsend[0]
        lsend[...] = packed
        larr[0] = packed
        acc1[...] = jnp.zeros((128, 256), F32)
        acc2[...] = jnp.zeros((128, 256), F32)

        def send_lower(i, carry):
            copy(lsend, larr.at[i], i, lsend_sem, lrecv).start()
            return carry

        lax.fori_loop(1, DEV, send_lower, 0)

        def gather_group(g, carry):
            wait_group(farr, g, fsend_sem, frecv, 1)
            highs, lows, highs01, lows01 = [], [], [], []
            for j in range(GROUP):
                i = g * GROUP + j
                d = source(i)
                m0, m1 = tab[3, d].astype(F32), tab[4, d].astype(F32)
                f = farr[i]
                highs.append(f.astype(BF16))
                high, low = split(jnp.concatenate([f * m0, f * m1], axis=1))
                highs01.append(high)
                lows01.append(low)
            high = jnp.concatenate(highs, axis=0)
            acc1[...] += mm(high, jnp.concatenate(highs01, axis=0), TN)
            acc2[...] += mm(high, jnp.concatenate(lows01, axis=0), TN)
            return carry

        lax.fori_loop(0, GROUPS, gather_group, 0)
        mu = jnp.where(index == 0, STEP_SIZES[0], jnp.where(index == 1, STEP_SIZES[1], jnp.where(index == 2, STEP_SIZES[2], STEP_SIZES[3]))).astype(F32)
        eye = (
            lax.broadcasted_iota(jnp.int32, (128, 128), 0) == lax.broadcasted_iota(jnp.int32, (128, 128), 1)
        ).astype(F32) * mu
        systems = []
        for t in range(2):
            cross = acc2[:, 128 * t : 128 * t + 128]
            systems.append(acc1[:, 128 * t : 128 * t + 128] + cross + cross.T + eye)
        a0, a1 = systems
        steps = [step_from(tab[5, 2 + t] // 2) for t in range(2)]
        b0, b1 = farr[steps[0]], farr[steps[1]]
        upper = jnp.where(left, a0[0:64], a1[64:128])
        under = jnp.where(left, a0[64:128], a1[0:64])
        solved = right_divide(rows_of(upper) + rows_of(under) + rows_of(jnp.where(half, b0, b1)))
        solved = jnp.concatenate(solved, axis=0)
        beside = jnp.concatenate([jnp.where(left, 0.0, a0[0:64]), jnp.where(left, a1[64:128], 0.0)], axis=0)
        update = mm_exact(solved, beside, NN)
        rest = jnp.where(left, a1[0:64], a0[64:128]) - update[0:64]
        side = jnp.where(half, b1, b0) - update[64:80]
        second = jnp.concatenate(right_divide(rows_of(rest) + rows_of(side))[0:2], axis=0)
        under = solved[0:64]
        back = jnp.concatenate([jnp.where(left, 0.0, under), jnp.where(left, under, 0.0)], axis=0)
        first = solved[64:80] - mm_exact(second, back, NN)
        answers = [jnp.where(half, first, second), jnp.where(half, second, first)]

        copies = copy(larr.at[pl.ds(1, DEV - 1)], larr.at[pl.ds(1, DEV - 1)], 1, lsend_sem, lrecv)
        copies.wait_recv()
        copies.wait_send()
        everyone = pl.ds(1, DEV - 1)
        copy(psend.at[everyone], parr.at[everyone], 1, psend_sem, precv.at[0]).wait_send()
        copy(fsend.at[everyone], farr.at[everyone], 1, fsend_sem, frecv.at[0]).wait_send()
        low16 = lanes() < 16
        for t in range(2):
            got = larr[steps[t]]
            got = jnp.where(tab[5, 2 + t] % 2 == 0, got, pltpu.roll(got, 64, 1))
            triangle = jnp.concatenate(
                [jnp.where(low16, got, 0.0), jnp.where(low16, pltpu.roll(got, 112, 1), 0.0)], axis=0
            )
            current[t] = mm_exact(triangle, answers[t], TN)[0:16]
        return carry

    lax.fori_loop(0, LAYERS, layer, 0)
    precoders_out[...] = current[...]


def tables(receiver_cells, transmitter_cells, interferers, counts):
    me = lax.axis_index("cells")
    linked = jnp.concatenate([receiver_cells[:, None], interferers], axis=1)
    in_use = jnp.arange(41, dtype=jnp.int32)[None, :] <= counts[:, None]
    mine = lax.dynamic_slice(linked, (2 * me, 0), (2, 41)).reshape(82)
    mine_use = lax.dynamic_slice(in_use, (2 * me, 0), (2, 41)).reshape(82)
    match = mine_use[:, None, None] & (mine[:, None, None] == transmitter_cells.reshape(1, DEV, 2))
    match = jnp.any(match, axis=2)
    number = jnp.arange(82, dtype=jnp.int32)[:, None]
    link = jnp.sum(jnp.where(match, number, 0), axis=0)
    apart = match & (number % 41 > 0)
    own0 = jnp.sum((apart & (number < 41)).astype(jnp.int32), axis=0)
    own1 = jnp.sum((apart & (number >= 41)).astype(jnp.int32), axis=0)
    cells = lax.dynamic_slice(transmitter_cells, (2 * me,), (2,))
    wanted = in_use[:, :, None] & (linked[:, :, None] == cells[None, None, :])
    wanted = jnp.any(jnp.any(wanted, axis=1).reshape(DEV, 2, 2), axis=1).astype(jnp.int32)
    place = jnp.arange(256, dtype=jnp.int32)
    heads = lax.dynamic_slice(receiver_cells, (2 * me,), (2,))
    from_device = jnp.sum(jnp.where(transmitter_cells[None, :] == heads[:, None], place[None, :] // 2, 0), axis=1)
    served = jnp.sum(jnp.where(receiver_cells[None, :] == cells[:, None], place[None, :], 0), axis=1)
    misc = jnp.concatenate([from_device, served, jnp.zeros((DEV - 4,), jnp.int32)])
    return jnp.stack([link, own0, own1, wanted[:, 0], wanted[:, 1], misc])


def body(channels, precoders_init, receiver_cells, transmitter_cells, interferers, counts):
    tab = tables(receiver_cells, transmitter_cells, interferers, counts)
    dma = pltpu.SemaphoreType.DMA
    precoders, weights = pl.pallas_call(
        kernel,
        out_shape=(
            jax.ShapeDtypeStruct((2, 16, 128), F32),
            jax.ShapeDtypeStruct((16, 128), F32),
        ),
        in_specs=[
            pl.BlockSpec(memory_space=pltpu.SMEM),
            pl.BlockSpec(memory_space=pl.ANY),
            pl.BlockSpec(memory_space=pltpu.VMEM),
        ],
        out_specs=(pl.BlockSpec(memory_space=pltpu.VMEM), pl.BlockSpec(memory_space=pltpu.VMEM)),
        scratch_shapes=[
            pltpu.VMEM((82, 64, 128), F32),
            pltpu.VMEM((82, 128, 128), BF16),
            pltpu.VMEM((2, 16, 128), F32),
            pltpu.VMEM((DEV, 16, 128), F32),
            pltpu.VMEM((DEV, 16, 128), F32),
            pltpu.VMEM((DEV, 16, 128), F32),
            pltpu.VMEM((DEV, 16, 128), F32),
            pltpu.VMEM((DEV, 16, 128), F32),
            pltpu.VMEM((8, 128), F32),
            pltpu.VMEM((DEV, 8, 128), F32),
            pltpu.VMEM((2, 32, 128), BF16),
            pltpu.VMEM((128, 256), F32),
            pltpu.VMEM((128, 256), F32),
            dma, dma, dma((GROUPS,)), dma, dma((GROUPS,)), dma, dma,
        ],
        compiler_params=pltpu.CompilerParams(collective_id=0, has_side_effects=True),
    )(tab, channels.reshape(82, 64, 128), precoders_init)
    weights = jnp.stack([weights[:, 0:16], weights[:, 64:80]]).reshape(2, 256)
    return (precoders, weights)


def solution(mesh):
    return jax.shard_map(
        body,
        mesh=mesh,
        in_specs=(P("cells", None, None, None), P("cells", None, None), P(), P(), P(), P()),
        out_specs=(P("cells", None, None), P("cells", None)),
        check_vma=False,
    )
```

time: 864 us -> 267 us (0.31); the launches traced: 853 us -> 266 us
  other arithmetic: 322 us -> 4.5 us
  waiting for transfers between devices: 275 us -> 0 us
  Pallas kernels: 0 us -> 255 us
  local copies, waits for them, and re-layouts: 119 us -> 5.88 us
  matrix products: 72.2 us -> 0 us
  starting transfers between devices: 49.9 us -> 0 us
  between operations: 15.1 us -> 0.73 us
    another operation x67 -> x2, other arithmetic: 296 us -> 0.67 us  [the longest x1 0.59 us: body(): weights = jnp.stack([weights[:, 0:16], weights[:, 64:80]]).reshape(2, 256)]
    pallas_call x0 -> x1, Pallas kernels: none -> 255 us  [body(): pl.pallas_call(kernel, out_shape=(jax.ShapeDtypeStruct((2, 16, 128), F32)...]
    all_gather x4 -> x0, waiting for transfers between devices: 188 us -> none  [body(): everything = lax.all_gather(precoders, 'cells', axis=0, tiled=True)]
    gather x17 -> x0, local copies, waits for them, and re-layouts: 87.4 us -> none  [the longest x5 61.7 us: link_tables(): positions = inverse[linked]]
    all_to_all x8 -> x0, waiting for transfers between devices: 86.3 us -> none  [the longest x4 64.3 us: body(): lax.all_to_all(outgoing_filters, 'cells', split_axis=0, concat_axis=0, ti...]
    dot_general x28 -> x0, matrix products: 64.5 us -> none  [the longest x4 21.5 us: receiver_step(): jnp.einsum('klrn,kldn->kldr', channels, link_precoders, precision=HIGHEST)]
    all_to_all x8 -> x0, starting transfers between devices: 49.8 us -> none  [the longest x4 28.9 us: body(): lax.all_to_all(link_weights.reshape(devices, capacity, streams * streams)...]
    mul x8 -> x0, local copies, waits for them, and re-layouts: 13.6 us -> none  [the longest x4 10.4 us: body(): selected = target_mask[:, :, None, None] * arrived[None]]
  transfers between devices with their start and end apart: 12 -> 0, of which waited for: 12 -> 0; matrix products, arithmetic and copies ran while one was open for 12% -> 0% of each run, Pallas kernels for 0% -> 0%
where the time goes in v1:
time: 267 us; the launch traced here: 266 us
  Pallas kernels  255 us (96%)
  local copies, waits for them, and re-layouts  5.88 us (2%)
  other arithmetic  4.5 us (2%)
    pallas_call x1, Pallas kernels, body(): pl.pallas_call(kernel, out_shape=(jax.ShapeDtypeStruct((2, 16, 128), F32)...  255 us

profile of v1, /device:TPU:1, one launch (start us, length us, event | category | flops | bytes accessed | tf_op | source)
XLA Modules:
  0.0 265.6 jit_solution(10688739413925433318)
XLA Ops:
  0.6 0.8 eq.60
  1.4 0.1 copy.13
  1.5 0.8 fusion
  2.3 0.1 copy.12
  2.4 0.1 eq.58
  2.5 0.8 iota_compare_fusion
  3.3 0.1 and.67
  3.4 0.1 and_reduce_fusion.1
  3.5 0.1 convert_reduce_fusion
  3.7 0.1 copy.14
  3.8 0.8 pad_add_fusion
  4.6 0.8 dynamic_slice.14
  5.3 0.2 and_reduce_fusion
  5.5 0.2 reshape.109
  5.7 0.1 reduce_or.29
  5.8 0.8 dynamic_slice.15
  6.6 0.9 fusion.1
  7.5 0.1 add_bitcast_fusion
  7.6 0.6 stack.28.tab
  8.2 254.5 %shard_map.77 = (f32[2,16,128]{2,1,0:T(8,128)}, f32[16,128]{1,0:T(8,128)}) custom-call(s32[6,128]{1,0:T(8,128)} %stack.28.tab, f32[82,64,128]{2,1,0:T(8,128)} %bitcast.13, f32[2,16,128]{2,1,0:T(8,128)} %first_precoders.1), custom_call_target="tpu_custom_call" | custom-call | tf_op jit(solution)/shard_map/pallas_call | solution.py:347
  262.7 0.8 fusion.4
  263.6 0.1 stack.30
  263.6 0.1 stack.29
  263.7 0.6 pad_maximum_fusion
  264.3 1.3 copy.18
  (7 shorter events, 0.0 us)

commit v2 on v1

--- a/solution.py
+++ b/solution.py
@@ -15,7 +15,11 @@
 DEV = 128
 GROUP = 16
 GROUPS = DEV // GROUP
-BLOCK = 8
+OFFSETS = sorted(
+    ((z, x, y, c) for z in range(4) for x in range(4) for y in range(4) for c in range(2)),
+    key=lambda o: -sum(min(a, 4 - a) for a in o[:3]) - 0.5 * o[3],
+)
+NUMBERS = [((z * 4 + x) * 4 + y) * 2 + c for z, x, y, c in OFFSETS]
 NN = (((1,), (0,)), ((), ()))
 NT = (((1,), (1,)), ((), ()))
 TN = (((0,), (0,)), ((), ()))
@@ -43,11 +47,7 @@
 
 
 def pick_lane(v, k):
-    return jnp.where(
-        lanes() < 64,
-        jnp.broadcast_to(v[:, k : k + 1], (8, 128)),
-        jnp.broadcast_to(v[:, 64 + k : 65 + k], (8, 128)),
-    )
+    return jnp.take_along_axis(v, jnp.where(lanes() < 64, k, 64 + k), axis=1)
 
 
 def rows_of(x):
@@ -56,26 +56,20 @@
 
 def right_divide(rows):
     rows = list(rows)
-    count = len(rows)
-    spot = lanes() % 64
-    for first in range(0, 64, BLOCK):
-        top = first // 8
-        columns = [{i: pick_lane(rows[i], first + j) for i in range(top, count)} for j in range(BLOCK)]
-        pivots = [pick_row(rows[top], j) for j in range(BLOCK)]
-        scaled = []
-        for j in range(BLOCK):
-            inverse = 1.0 / pick_row(columns[j][top], j)
-            row = (pivots[j] - (spot == first + j).astype(F32)) * inverse
-            scaled.append(row)
-            for later in range(j + 1, BLOCK):
-                factor = pick_row(columns[later][top], j) * inverse
-                for i in range(top, count):
-                    columns[later][i] = columns[later][i] - columns[j][i] * factor
-                pivots[later] = pivots[later] - pick_row(columns[j][top], later) * row
-        for i in range(top, count):
+    spot, line = lanes() % 64, lax.broadcasted_iota(jnp.int32, (8, 128), 0)
+    for top in range(8):
+        columns = [pick_lane(rows[top], 8 * top + j) for j in range(8)]
+        x = rows[top] - (spot == line + 8 * top).astype(F32)
+        for j in range(8):
+            factor = (columns[j] - (line == j).astype(F32)) * (1.0 / pick_row(columns[j], j))
+            for later in range(j + 1, 8):
+                columns[later] = columns[later] - factor * pick_row(columns[later], j)
+            x = x - factor * pick_row(x, j)
+        pivots = [pick_row(x, j) for j in range(8)]
+        for i in range(top + 1, len(rows)):
             total = rows[i]
-            for j in range(BLOCK):
-                total = total - columns[j][i] * scaled[j]
+            for j in range(8):
+                total = total - pick_lane(rows[i], 8 * top + j) * pivots[j]
             rows[i] = total
     return rows[8:]
 
@@ -84,17 +78,21 @@
     ws, vs = rows_of(w), rows_of(v)
     line = lax.broadcasted_iota(jnp.int32, (8, 128), 0)
     diagonal = [jnp.ones((8, 128), F32), jnp.ones((8, 128), F32)]
-    for k in range(16):
-        top, at = divmod(k, 8)
-        columns = {i: pick_lane(ws[i], k) for i in range(top, 2)}
-        pivot = pick_row(columns[top], at)
-        inverse = 1.0 / pivot
-        wrow, vrow = pick_row(ws[top], at) * inverse, pick_row(vs[top], at) * inverse
-        diagonal[top] = jnp.where(line == at, pivot, diagonal[top])
-        for i in range(top, 2):
-            column = jnp.where(line > at, columns[i], 0.0) if i == top else columns[i]
-            ws[i] = ws[i] - column * wrow
-            vs[i] = vs[i] - column * vrow
+    for top in range(2):
+        columns = [[pick_lane(ws[i], 8 * top + j) for i in range(top, 2)] for j in range(8)]
+        for j in range(8):
+            pivot = pick_row(columns[j][0], j)
+            inverse = 1.0 / pivot
+            factors = [c * inverse for c in columns[j]]
+            factors[0] = jnp.where(line > j, factors[0], 0.0)
+            diagonal[top] = jnp.where(line == j, pivot, diagonal[top])
+            for later in range(j + 1, 8):
+                row = pick_row(columns[later][0], j)
+                columns[later] = [c - f * row for c, f in zip(columns[later], factors)]
+            wrow, vrow = pick_row(ws[top], j), pick_row(vs[top], j)
+            for i in range(top, 2):
+                ws[i] = ws[i] - factors[i - top] * wrow
+                vs[i] = vs[i] - factors[i - top] * vrow
     out_l, out_v = [], []
     for i in range(2):
         scale = 1.0 / jnp.sqrt(diagonal[i])
@@ -112,17 +110,23 @@
     me = lax.axis_index("cells")
     mz, mx, my, mc = me // 32, (me // 8) % 4, (me // 2) % 4, me % 2
 
-    def target(i):
-        dz, dx, dy, dc = i // 32, (i // 8) % 4, (i // 2) % 4, i % 2
-        return (((mz + dz) % 4 * 4 + (mx + dx) % 4) * 4 + (my + dy) % 4) * 2 + (mc + dc) % 2
-
-    def source(i):
-        dz, dx, dy, dc = i // 32, (i // 8) % 4, (i // 2) % 4, i % 2
-        return (((mz + 4 - dz) % 4 * 4 + (mx + 4 - dx) % 4) * 4 + (my + 4 - dy) % 4) * 2 + (mc + 2 - dc) % 2
+    zs = [lax.rem(mz + a, 4) * 32 for a in range(4)]
+    xs = [lax.rem(mx + a, 4) * 8 for a in range(4)]
+    ys = [lax.rem(my + a, 4) * 2 for a in range(4)]
+    cs = [mc, 1 - mc]
+
+    def target(k):
+        dz, dx, dy, dc = OFFSETS[k]
+        return zs[dz] + xs[dx] + ys[dy] + cs[dc]
+
+    def source(k):
+        dz, dx, dy, dc = OFFSETS[k]
+        return zs[(4 - dz) % 4] + xs[(4 - dx) % 4] + ys[(4 - dy) % 4] + cs[dc]
 
     def step_from(d):
         z, x, y, c = d // 32, (d // 8) % 4, (d // 2) % 4, d % 2
-        return (((mz + 4 - z) % 4 * 4 + (mx + 4 - x) % 4) * 4 + (my + 4 - y) % 4) * 2 + (mc + 2 - c) % 2
+        number = (((mz + 4 - z) % 4 * 4 + (mx + 4 - x) % 4) * 4 + (my + 4 - y) % 4) * 2 + (mc + 2 - c) % 2
+        return tab[6, number]
 
     def copy(src, dst, i, send, recv):
         return pltpu.make_async_remote_copy(
@@ -130,31 +134,21 @@
             device_id=(target(i),), device_id_type=MESH,
         )
 
-    def wait_group(buf, g, send, recv, first):
-        @pl.when(g == 0)
-        def _():
-            part = buf.at[pl.ds(1, GROUP - 1)]
-            copy(part, part, 1, send, recv.at[0]).wait_recv()
-
-        @pl.when(g > 0)
-        def _():
-            part = buf.at[pl.ds(g * GROUP, GROUP)]
-            copy(part, part, 1, send, recv.at[g]).wait_recv()
+    remote = pl.ds(0, DEV - 1)
+
+    def wait_group(buf, g, send, recv):
+        part = buf.at[pl.ds(g * GROUP, GROUP - 1 if g == GROUPS - 1 else GROUP)]
+        copy(part, part, 0, send, recv.at[g]).wait_recv()
 
     fetch = pltpu.make_async_copy(channels, raw, raw_sem)
     fetch.start()
     barrier = pltpu.get_barrier_semaphore()
 
-    def greet(i, carry):
-        pl.semaphore_signal(barrier, inc=1, device_id=(target(i),), device_id_type=MESH)
-        return carry
-
-    lax.fori_loop(1, DEV, greet, 0)
+    for k in range(DEV - 1):
+        pl.semaphore_signal(barrier, inc=1, device_id=(target(k),), device_id_type=MESH)
     current[...] = first_precoders[...]
     half = lax.broadcasted_iota(jnp.int32, (16, 128), 1) < 64
     left = lax.broadcasted_iota(jnp.int32, (64, 128), 1) < 64
-    pl.semaphore_wait(barrier, DEV - 1)
-    fetch.wait()
 
     def prepare(i, carry):
         high, low = split(raw[i])
@@ -162,32 +156,25 @@
         links[i, 64:128, :] = low
         return carry
 
+    fetch.wait()
+    lax.fori_loop(0, 82, prepare, 0)
+    pl.semaphore_wait(barrier, DEV - 1)
+
     def layer(index, carry):
-        def select(i, carry):
-            psend[i] = current[tab[4, target(i)]]
-            return carry
-
-        lax.fori_loop(0, DEV, select, 0, unroll=8)
-        parr[0] = psend[0]
-
-        def send_precoder(i, carry):
-            copy(psend.at[i], parr.at[i], i, psend_sem, precv.at[i // GROUP]).start()
-            return carry
-
-        lax.fori_loop(1, DEV, send_precoder, 0)
-
-        @pl.when(index == 0)
-        def _():
-            lax.fori_loop(0, 82, prepare, 0)
+        for g in range(GROUPS):
+            for k in range(g * GROUP, g * GROUP + GROUP):
+                psend[k] = current[tab[4, target(k)]]
+            for k in range(g * GROUP, min(g * GROUP + GROUP, DEV - 1)):
+                copy(psend.at[k], parr.at[k], k, psend_sem, precv.at[g]).start()
+        parr[DEV - 1] = psend[DEV - 1]
 
         acc1[...] = jnp.zeros((128, 256), F32)
         acc2[...] = jnp.zeros((128, 256), F32)
 
-        def images(g, carry):
-            wait_group(parr, g, psend_sem, precv, 1)
+        for g in range(GROUPS):
+            wait_group(parr, g, psend_sem, precv)
             highs, lows = [], []
-            for j in range(GROUP):
-                i = g * GROUP + j
+            for i in range(g * GROUP, g * GROUP + GROUP):
                 d = source(i)
                 high, low = split(parr[i])
                 product = mm(jnp.concatenate([high, low], axis=0), links[tab[0, d]], NT)
@@ -201,9 +188,7 @@
             high, low = jnp.concatenate(highs, axis=0), jnp.concatenate(lows, axis=0)
             acc1[:, 0:128] += mm(high, high, TN)
             acc2[:, 0:128] += mm(high, low, TN)
-            return carry
-
-        lax.fori_loop(0, GROUPS, images, 0)
+
         cross = acc2[:, 0:128]
         full = acc1[:, 0:128] + cross + cross.T
         line = lax.broadcasted_iota(jnp.int32, (64, 128), 0)
@@ -225,40 +210,31 @@
             mine = mine + pltpu.roll(mine, 64, 1)
             high, low = split(mine)
             pair[s] = jnp.concatenate([high, low], axis=0)
-        packed = lower[0] + pltpu.roll(lower[1], 16, 1)
-
-        def filter_group(g, carry):
-            for j in range(GROUP):
-                i = g * GROUP + j
-                at = tab[0, target(i)]
-                product = mm(pair[at // 41], links[at], NN)
-                fsend[i] = product[0:16] + product[16:32]
-
-            def send_filter(i, carry):
-                copy(fsend.at[i], farr.at[i], i, fsend_sem, frecv.at[i // GROUP]).start()
-                return carry
-
-            lax.fori_loop(jnp.where(g == 0, 1, g * GROUP), (g + 1) * GROUP, send_filter, 0)
-            return carry
-
-        lax.fori_loop(0, GROUPS, filter_group, 0)
-        farr[0] = fsend[0]
-        lsend[...] = packed
-        larr[0] = packed
+        for s in range(2):
+            for i in range(2):
+                part = lower[i] if s == 0 else pltpu.roll(lower[i], 64, 1)
+                part = pltpu.roll(jnp.where(lanes() < 16, part, 0.0), 0, 1, stride=16, stride_axis=0)
+                lsend[2 * s + i : 2 * s + i + 1, :] = jnp.sum(part, axis=0, keepdims=True)
+        larr[DEV - 1] = lsend[...]
+
+        for g in range(GROUPS):
+            for k in range(g * GROUP, g * GROUP + GROUP):
+                d = target(k)
+                product = mm(pair[tab[7, d]], links[tab[0, d]], NN)
+                fsend[k] = product[0:16] + product[16:32]
+            for k in range(g * GROUP, min(g * GROUP + GROUP, DEV - 1)):
+                copy(fsend.at[k], farr.at[k], k, fsend_sem, frecv.at[g]).start()
+        farr[DEV - 1] = fsend[DEV - 1]
         acc1[...] = jnp.zeros((128, 256), F32)
         acc2[...] = jnp.zeros((128, 256), F32)
 
-        def send_lower(i, carry):
-            copy(lsend, larr.at[i], i, lsend_sem, lrecv).start()
-            return carry
-
-        lax.fori_loop(1, DEV, send_lower, 0)
-
-        def gather_group(g, carry):
-            wait_group(farr, g, fsend_sem, frecv, 1)
+        for k in range(DEV - 1):
+            copy(lsend, larr.at[k], k, lsend_sem, lrecv).start()
+
+        for g in range(GROUPS):
+            wait_group(farr, g, fsend_sem, frecv)
             highs, lows, highs01, lows01 = [], [], [], []
-            for j in range(GROUP):
-                i = g * GROUP + j
+            for i in range(g * GROUP, g * GROUP + GROUP):
                 d = source(i)
                 m0, m1 = tab[3, d].astype(F32), tab[4, d].astype(F32)
                 f = farr[i]
@@ -269,9 +245,7 @@
             high = jnp.concatenate(highs, axis=0)
             acc1[...] += mm(high, jnp.concatenate(highs01, axis=0), TN)
             acc2[...] += mm(high, jnp.concatenate(lows01, axis=0), TN)
-            return carry
-
-        lax.fori_loop(0, GROUPS, gather_group, 0)
+
         mu = jnp.where(index == 0, STEP_SIZES[0], jnp.where(index == 1, STEP_SIZES[1], jnp.where(index == 2, STEP_SIZES[2], STEP_SIZES[3]))).astype(F32)
         eye = (
             lax.broadcasted_iota(jnp.int32, (128, 128), 0) == lax.broadcasted_iota(jnp.int32, (128, 128), 1)
@@ -297,18 +271,22 @@
         first = solved[64:80] - mm_exact(second, back, NN)
         answers = [jnp.where(half, first, second), jnp.where(half, second, first)]
 
-        copies = copy(larr.at[pl.ds(1, DEV - 1)], larr.at[pl.ds(1, DEV - 1)], 1, lsend_sem, lrecv)
-        copies.wait_recv()
-        copies.wait_send()
-        everyone = pl.ds(1, DEV - 1)
-        copy(psend.at[everyone], parr.at[everyone], 1, psend_sem, precv.at[0]).wait_send()
-        copy(fsend.at[everyone], farr.at[everyone], 1, fsend_sem, frecv.at[0]).wait_send()
+        lowers = copy(larr.at[remote], larr.at[remote], 0, lsend_sem, lrecv)
+        lowers.wait_recv()
+        lowers.wait_send()
+        copy(psend.at[remote], parr.at[remote], 0, psend_sem, precv.at[0]).wait_send()
+        copy(fsend.at[remote], farr.at[remote], 0, fsend_sem, frecv.at[0]).wait_send()
         low16 = lanes() < 16
+        unpack = (lanes() + 16 * lax.broadcasted_iota(jnp.int32, (8, 128), 0)) % 128
         for t in range(2):
             got = larr[steps[t]]
-            got = jnp.where(tab[5, 2 + t] % 2 == 0, got, pltpu.roll(got, 64, 1))
+            got = jnp.where(tab[5, 2 + t] % 2 == 0, got[0:2], got[2:4])
             triangle = jnp.concatenate(
-                [jnp.where(low16, got, 0.0), jnp.where(low16, pltpu.roll(got, 112, 1), 0.0)], axis=0
+                [
+                    jnp.where(low16, jnp.take_along_axis(pick_row(got, i), unpack, axis=1), 0.0)
+                    for i in range(2)
+                ],
+                axis=0,
             )
             current[t] = mm_exact(triangle, answers[t], TN)[0:16]
         return carry
@@ -338,7 +316,10 @@
     from_device = jnp.sum(jnp.where(transmitter_cells[None, :] == heads[:, None], place[None, :] // 2, 0), axis=1)
     served = jnp.sum(jnp.where(receiver_cells[None, :] == cells[:, None], place[None, :], 0), axis=1)
     misc = jnp.concatenate([from_device, served, jnp.zeros((DEV - 4,), jnp.int32)])
-    return jnp.stack([link, own0, own1, wanted[:, 0], wanted[:, 1], misc])
+    order = jnp.asarray(NUMBERS, jnp.int32)
+    position = jnp.sum(jnp.where(order[:, None] == jnp.arange(DEV)[None, :], jnp.arange(DEV)[:, None], 0), axis=0)
+    second = jnp.any(match & (number >= 41), axis=0).astype(jnp.int32)
+    return jnp.stack([link, own0, own1, wanted[:, 0], wanted[:, 1], misc, position, second])
 
 
 def body(channels, precoders_init, receiver_cells, transmitter_cells, interferers, counts):
@@ -365,8 +346,8 @@
             pltpu.VMEM((DEV, 16, 128), F32),
             pltpu.VMEM((DEV, 16, 128), F32),
             pltpu.VMEM((DEV, 16, 128), F32),
-            pltpu.VMEM((8, 128), F32),
-            pltpu.VMEM((DEV, 8, 128), F32),
+            pltpu.VMEM((4, 128), F32),
+            pltpu.VMEM((DEV, 4, 128), F32),
             pltpu.VMEM((2, 32, 128), BF16),
             pltpu.VMEM((128, 256), F32),
             pltpu.VMEM((128, 256), F32),

time: 267 us -> 192 us (0.72)
  Pallas kernels: 255 us -> 180 us
    pallas_call x1, Pallas kernels: 255 us -> 180 us  [body(): pl.pallas_call(kernel, out_shape=(jax.ShapeDtypeStruct((2, 16, 128), F32)...]
where the time goes in v2:
time: 192 us
  Pallas kernels  180 us (94%)
  local copies, waits for them, and re-layouts  5.88 us (3%)
  other arithmetic  5.36 us (3%)
    pallas_call x1, Pallas kernels, body(): pl.pallas_call(kernel, out_shape=(jax.ShapeDtypeStruct((2, 16, 128), F32)...  180 us

profile of v2, /device:TPU:1, one launch (start us, length us, event | category | flops | bytes accessed | tf_op | source)
XLA Modules:
  0.0 192.2 jit_solution(5696316428543437655)
XLA Ops:
  0.6 0.8 dynamic_slice.14
  1.4 0.8 select_reduce_fusion
  2.1 0.8 dynamic_slice.15
  2.9 0.9 fusion.1
  3.8 0.1 add_bitcast_fusion
  3.9 0.8 fusion
  4.7 0.1 copy.13
  4.8 0.1 eq.36
  4.9 0.8 iota_compare_fusion
  5.7 0.1 copy.15
  5.8 0.1 and.75
  5.9 0.8 pad_add_fusion
  6.7 0.2 and_reduce_fusion
  6.9 0.2 reshape.119
  7.0 0.1 reduce_or.38
  7.2 0.8 eq.73
  8.0 0.1 copy.14
  8.1 0.1 and_reduce_fusion.1
  8.2 0.1 and_reduce_fusion.2
  8.3 0.1 convert_reduce_fusion
  8.4 0.6 stack.33.tab
  9.0 180.2 %shard_map.86 = (f32[2,16,128]{2,1,0:T(8,128)}, f32[16,128]{1,0:T(8,128)}) custom-call(s32[8,128]{1,0:T(8,128)} %stack.33.tab, f32[82,64,128]{2,1,0:T(8,128)} %bitcast.16, f32[2,16,128]{2,1,0:T(8,128)} %first_precoders.1), custom_call_target="tpu_custom_call" | custom-call | tf_op jit(solution)/shard_map/pallas_call | solution.py:328
  189.3 0.8 fusion.4
  190.1 0.1 stack.34
  190.2 0.1 stack.35
  190.3 0.6 pad_maximum_fusion
  190.9 1.3 copy.19
  (8 shorter events, 0.0 us)

commit v3 on v2

v3 whole, which is shorter than its diff:
```python
import random

import jax
import jax.numpy as jnp
from jax import lax
from jax.experimental import pallas as pl
from jax.experimental.pallas import tpu as pltpu
from jax.sharding import PartitionSpec as P

LAYERS = 4
STEP_SIZES = (0.3, 0.2, 0.15, 0.1)
HIGHEST = lax.Precision.HIGHEST
MESH = pl.DeviceIdType.MESH
F32, BF16 = jnp.float32, jnp.bfloat16
DEV = 128
OFFSETS = [(z, x, y, c) for z in range(4) for x in range(4) for y in range(4) for c in range(2)]
shuffled = random.Random(5)
ORDER = sorted(range(DEV), key=lambda i: (-sum(min(a, 4 - a) for a in OFFSETS[i][:3]), -i if i < 2 else shuffled.random()))
SIZES = [8, 8, 16, 16, 16, 16, 16, 16, 8, 8]
GROUPS = [ORDER[sum(SIZES[:g]) : sum(SIZES[: g + 1])] for g in range(len(SIZES))]
LAST = len(GROUPS) - 1
LATE = 7
NN = (((1,), (0,)), ((), ()))
NT = (((1,), (1,)), ((), ()))
TN = (((0,), (0,)), ((), ()))


def split(x):
    high = x.astype(BF16)
    return high, (x - high.astype(F32)).astype(BF16)


def mm(a, b, dims):
    return lax.dot_general(a, b, dims, preferred_element_type=F32)


def mm_exact(a, b, dims):
    return lax.dot_general(a, b, dims, precision=HIGHEST, preferred_element_type=F32)


def mm_split(a, b, dims):
    (ah, al), (bh, bl) = split(a), split(b)
    return mm(ah, bh, dims) + (mm(ah, bl, dims) + mm(al, bh, dims))


def lanes():
    return lax.broadcasted_iota(jnp.int32, (8, 128), 1)


def pick_row(v, row):
    return jnp.broadcast_to(v[row : row + 1, :], (8, 128))


def pick_lane(v, k):
    return jnp.take_along_axis(v, jnp.where(lanes() < 64, k, 64 + k), axis=1)


def rows_of(x):
    return [x[8 * i : 8 * i + 8, :] for i in range(x.shape[0] // 8)]


def clear_block(rows, top, others):
    spot, line = lanes() % 64, lax.broadcasted_iota(jnp.int32, (8, 128), 0)
    columns = [pick_lane(rows[top], 8 * top + j) for j in range(8)]
    unit = (spot == line + 8 * top).astype(F32)
    x = rows[top] - unit
    for j in range(0, 8, 2):
        a, b = columns[j], columns[j + 1]
        p11, p21, p12, p22 = pick_row(a, j), pick_row(a, j + 1), pick_row(b, j), pick_row(b, j + 1)
        inverse = 1.0 / (p11 * p22 - p12 * p21)
        a, b = a - (line == j).astype(F32), b - (line == j + 1).astype(F32)
        one, two = (a * p22 - b * p21) * inverse, (b * p11 - a * p12) * inverse
        for later in range(j + 2, 8):
            column = columns[later]
            columns[later] = column - one * pick_row(column, j) - two * pick_row(column, j + 1)
        x = x - one * pick_row(x, j) - two * pick_row(x, j + 1)
    pivots = [pick_row(x, j) for j in range(8)]
    for i in others:
        t = [pick_lane(rows[i], 8 * top + j) * pivots[j] for j in range(8)]
        rows[i] = rows[i] - (((t[0] + t[1]) + (t[2] + t[3])) + ((t[4] + t[5]) + (t[6] + t[7])))
    rows[top] = unit - x


def right_divide(rows):
    rows = list(rows)
    for top in range(8):
        clear_block(rows, top, range(top + 1, len(rows)))
    return rows[8:]


def invert(rows):
    rows = list(rows)
    for top in range(8):
        clear_block(rows, top, [i for i in range(8) if i != top])
    return jnp.concatenate(rows, axis=0)


def lower_divide(w, v):
    ws, vs = rows_of(w), rows_of(v)
    line = lax.broadcasted_iota(jnp.int32, (8, 128), 0)
    diagonal = [jnp.ones((8, 128), F32), jnp.ones((8, 128), F32)]
    for top in range(2):
        columns = [[pick_lane(ws[i], 8 * top + j) for i in range(top, 2)] for j in range(8)]
        for j in range(8):
            pivot = pick_row(columns[j][0], j)
            inverse = 1.0 / pivot
            factors = [c * inverse for c in columns[j]]
            factors[0] = jnp.where(line > j, factors[0], 0.0)
            diagonal[top] = jnp.where(line == j, pivot, diagonal[top])
            for later in range(j + 1, 8):
                row = pick_row(columns[later][0], j)
                columns[later] = [c - f * row for c, f in zip(columns[later], factors)]
            wrow, vrow = pick_row(ws[top], j), pick_row(vs[top], j)
            for i in range(top, 2):
                ws[i] = ws[i] - factors[i - top] * wrow
                vs[i] = vs[i] - factors[i - top] * vrow
    out_l, out_v = [], []
    for i in range(2):
        scale = 1.0 / jnp.sqrt(diagonal[i])
        keep = (lanes() % 64 >= line + 8 * i) & (lanes() % 64 < 16)
        out_l.append(jnp.where(keep, ws[i] * scale, 0.0))
        out_v.append(vs[i] * scale)
    return out_l, jnp.concatenate(out_v, axis=0)


def pack_rows(top, bottom, s):
    out = []
    for part in (top, bottom):
        part = part if s == 0 else pltpu.roll(part, 64, 1)
        part = pltpu.roll(jnp.where(lanes() < 16, part, 0.0), 0, 1, stride=16, stride_axis=0)
        out.append(jnp.sum(part, axis=0, keepdims=True))
    return out


def make_table(me, receivers, transmitters, counts, interferers):
    lane = lax.broadcasted_iota(jnp.int32, (1, 256), 1)
    listed = interferers
    number = lax.broadcasted_iota(jnp.int32, (40, 256), 0)
    used = number < counts
    link, apart, slots, wanted, served = jnp.zeros((1, 256), jnp.int32), [], [], [], []
    for s in range(2):
        mine = lane == 2 * me + s
        cell = jnp.sum(jnp.where(mine, receivers, 0), axis=1, keepdims=True)
        column = jnp.max(jnp.where(mine & used, listed, -1), axis=1, keepdims=True)
        match = (column == transmitters).astype(jnp.int32)
        own = (cell == transmitters).astype(jnp.int32)
        apart.append(jnp.sum(match, axis=0, keepdims=True))
        link = link + jnp.sum(match * (number + (1 + 41 * s)), axis=0, keepdims=True) + own * (41 * s)
        slots.append(jnp.sum(own * lane, axis=1, keepdims=True))
        if s == 1:
            second = apart[1] + own
        cell = jnp.sum(jnp.where(mine, transmitters, 0), axis=1, keepdims=True)
        own = (cell == receivers).astype(jnp.int32)
        wanted.append(jnp.max((used & (listed == cell)).astype(jnp.int32), axis=0, keepdims=True) + own)
        served.append(jnp.sum(own * lane, axis=1, keepdims=True))
    misc = sum(jnp.where(lane == i, v, 0) for i, v in enumerate(slots + served))
    rows = [link, apart[0], apart[1], wanted[0], wanted[1], second]
    rows = [r + pltpu.roll(r, 255, 1) for r in rows] + [misc, misc]
    return [jnp.clip(r, 0, top) for r, top in zip(rows, (81, 1, 1, 1, 1, 1, 255, 255))]


def kernel(
    receivers, transmitters, counts, interferers, channels, first_precoders, precoders_out, weights_out,
    raw, links, current, psend, parr, gbuf, fsend, farr, lsend, larr, pair, acc1, acc2, tabv, tab,
    raw_sem, tab_sem, psend_sem, precv, fsend_sem, frecv, lsend_sem, lrecv,
):
    me = lax.axis_index("cells")
    mz, mx, my, mc = me // 32, (me // 8) % 4, (me // 2) % 4, me % 2

    zs = [lax.rem(mz + a, 4) * 32 for a in range(4)]
    xs = [lax.rem(mx + a, 4) * 8 for a in range(4)]
    ys = [lax.rem(my + a, 4) * 2 for a in range(4)]
    cs = [mc, 1 - mc]

    def target(k):
        dz, dx, dy, dc = OFFSETS[k]
        return zs[dz] + xs[dx] + ys[dy] + cs[dc]

    def source(k):
        dz, dx, dy, dc = OFFSETS[k]
        return zs[(4 - dz) % 4] + xs[(4 - dx) % 4] + ys[(4 - dy) % 4] + cs[dc]

    def slot_from(d):
        z, x, y, c = d // 32, (d // 8) % 4, (d // 2) % 4, d % 2
        return (((mz + 4 - z) % 4 * 4 + (mx + 4 - x) % 4) * 4 + (my + 4 - y) % 4) * 2 + (mc + 2 - c) % 2

    def copy(src, dst, i, send, recv):
        return pltpu.make_async_remote_copy(
            src_ref=src, dst_ref=dst, send_sem=send, recv_sem=recv,
            device_id=(target(i),), device_id_type=MESH,
        )

    remote = pl.ds(1, DEV - 1)

    def wait_group(buf, g, send, recv):
        part = buf.at[pl.ds(1, SIZES[g] - (g == LAST))]
        copy(part, part, ORDER[0], send, recv.at[g]).wait_recv()

    fetch = pltpu.make_async_copy(channels, raw, raw_sem)
    fetch.start()
    barrier = pltpu.get_barrier_semaphore()

    for k in ORDER[: DEV - 1]:
        pl.semaphore_signal(barrier, inc=1, device_id=(target(k),), device_id_type=MESH)
    current[...] = first_precoders[...]
    table = make_table(me, receivers[...], transmitters[...], counts[...], interferers[...])
    for i in range(8):
        tabv[i : i + 1, :] = table[i]
    lookup = pltpu.make_async_copy(tabv, tab, tab_sem)
    lookup.start()
    half = lax.broadcasted_iota(jnp.int32, (16, 128), 1) < 64
    left = lax.broadcasted_iota(jnp.int32, (64, 128), 1) < 64

    def prepare(i, carry):
        high, low = split(raw[i])
        links[i, 0:64, :] = high
        links[i, 64:128, :] = low
        return carry

    fetch.wait()
    lax.fori_loop(0, 82, prepare, 0)
    lookup.wait()
    pl.semaphore_wait(barrier, DEV - 1)

    def layer(index, carry):
        for g, members in enumerate(GROUPS):
            for k in members:
                psend[k] = current[tab[4, 2 * target(k)]]
            for k in members:
                if k > 0:
                    copy(psend.at[k], parr.at[k], k, psend_sem, precv.at[g]).start()
        parr[0] = psend[0]

        for g, members in enumerate(GROUPS):
            wait_group(parr, g, psend_sem, precv)
            highs, lows = [], []
            for i in members:
                d = source(i)
                high, low = split(parr[i])
                product = mm(jnp.concatenate([high, low], axis=0), links[tab[0, 2 * d]], NT)
                total = product[0:16] + product[16:32]
                total = total + pltpu.roll(total, 64, 1)
                gbuf[i] = total
                masked = total * jnp.where(half, tab[1, 2 * d].astype(F32), tab[2, 2 * d].astype(F32))
                high, low = split(masked)
                highs.append(high)
                lows.append(low)
            high, low = jnp.concatenate(highs, axis=0), jnp.concatenate(lows, axis=0)
            one, two = mm(high, high, TN), mm(high, low, TN)
            acc1[:, 0:128] = one if g == 0 else acc1[:, 0:128] + one
            acc2[:, 0:128] = two if g == 0 else acc2[:, 0:128] + two

        cross = acc2[:, 0:128]
        full = acc1[:, 0:128] + cross + cross.T
        line = lax.broadcasted_iota(jnp.int32, (64, 128), 0)
        spot = lax.broadcasted_iota(jnp.int32, (64, 128), 1) % 64
        covariance = jnp.where(left, full[0:64], full[64:128]) + (line == spot).astype(F32)
        direct = jnp.where(half, gbuf[slot_from(tab[6, 0] // 2)], gbuf[slot_from(tab[6, 1] // 2)])
        v = jnp.concatenate(right_divide(rows_of(covariance) + rows_of(direct))[0:2], axis=0)
        blank = jnp.zeros((48, 128), F32)
        apart = jnp.concatenate(
            [jnp.where(half, direct, 0.0), blank, jnp.where(half, 0.0, direct), blank], axis=0
        )
        short = lax.broadcasted_iota(jnp.int32, (16, 128), 0)
        w = mm_exact(v, apart, NT)
        w = w + (lax.broadcasted_iota(jnp.int32, (16, 128), 1) % 64 == short).astype(F32)
        for s in range(2):
            for i, row in enumerate(pack_rows(w[0:8], w[8:16], s)):
                weights_out[s : s + 1, 128 * i : 128 * i + 128] = row
        lower, filters = lower_divide(w, v)
        for s in range(2):
            mine = jnp.where(half, filters, 0.0) if s == 0 else jnp.where(half, 0.0, filters)
            mine = mine + pltpu.roll(mine, 64, 1)
            high, low = split(mine)
            pair[s] = jnp.concatenate([high, low], axis=0)
        for s in range(2):
            for i, row in enumerate(pack_rows(lower[0], lower[1], s)):
                lsend[2 * s + i : 2 * s + i + 1, :] = row
        larr[0] = lsend[...]

        for g, members in enumerate(GROUPS):
            for k in members:
                d = 2 * target(k)
                product = mm(pair[tab[5, d]], links[tab[0, d]], NN)
                fsend[k] = product[0:16] + product[16:32]
            for k in members:
                if k > 0:
                    copy(fsend.at[k], farr.at[k], k, fsend_sem, frecv.at[g]).start()
        farr[0] = fsend[0]

        for g, members in enumerate(GROUPS):
            if g == LATE:
                for k in ORDER[: DEV - 1]:
                    copy(lsend, larr.at[k], k, lsend_sem, lrecv).start()
            wait_group(farr, g, fsend_sem, frecv)
            highs, lows, highs01, lows01 = [], [], [], []
            for i in members:
                d = source(i)
                m0, m1 = tab[3, 2 * d].astype(F32), tab[4, 2 * d].astype(F32)
                f = farr[i]
                highs.append(f.astype(BF16))
                high, low = split(jnp.concatenate([f * m0, f * m1], axis=1))
                highs01.append(high)
                lows01.append(low)
            high = jnp.concatenate(highs, axis=0)
            one = mm(high, jnp.concatenate(highs01, axis=0), TN)
            two = mm(high, jnp.concatenate(lows01, axis=0), TN)
            acc1[...] = one if g == 0 else acc1[...] + one
            acc2[...] = two if g == 0 else acc2[...] + two

        mu = jnp.where(index == 0, STEP_SIZES[0], jnp.where(index == 1, STEP_SIZES[1], jnp.where(index == 2, STEP_SIZES[2], STEP_SIZES[3]))).astype(F32)
        eye = (
            lax.broadcasted_iota(jnp.int32, (128, 128), 0) == lax.broadcasted_iota(jnp.int32, (128, 128), 1)
        ).astype(F32) * mu
        systems = []
        for t in range(2):
            cross = acc2[:, 128 * t : 128 * t + 128]
            systems.append(acc1[:, 128 * t : 128 * t + 128] + cross + cross.T + eye)
        a0, a1 = systems
        steps = [slot_from(tab[6, 2 + t] // 2) for t in range(2)]
        b0, b1 = farr[steps[0]], farr[steps[1]]
        upper = jnp.where(left, a0[0:64], a1[64:128])
        under = jnp.where(left, a0[64:128], a1[0:64])
        inverse = invert(rows_of(upper))
        diagonal = jnp.concatenate([jnp.where(left, inverse, 0.0), jnp.where(left, 0.0, inverse)], axis=0)
        solved = mm_split(jnp.concatenate([under, jnp.where(half, b0, b1)], axis=0), diagonal, NN)
        beside = jnp.concatenate([jnp.where(left, 0.0, a0[0:64]), jnp.where(left, a1[64:128], 0.0)], axis=0)
        update = mm_split(solved, beside, NN)
        rest = jnp.where(left, a1[0:64], a0[64:128]) - update[0:64]
        side = jnp.where(half, b1, b0) - update[64:80]
        second = jnp.concatenate(right_divide(rows_of(rest) + rows_of(side))[0:2], axis=0)
        under = solved[0:64]
        back = jnp.concatenate([jnp.where(left, 0.0, under), jnp.where(left, under, 0.0)], axis=0)
        first = solved[64:80] - mm_split(second, back, NN)
        answers = [jnp.where(half, first, second), jnp.where(half, second, first)]

        lowers = copy(larr.at[remote], larr.at[remote], ORDER[0], lsend_sem, lrecv)
        lowers.wait_recv()
        lowers.wait_send()
        copy(psend.at[remote], parr.at[remote], ORDER[0], psend_sem, precv.at[0]).wait_send()
        copy(fsend.at[remote], farr.at[remote], ORDER[0], fsend_sem, frecv.at[0]).wait_send()
        low16 = lanes() < 16
        unpack = (lanes() + 16 * lax.broadcasted_iota(jnp.int32, (8, 128), 0)) % 128
        for t in range(2):
            got = larr[steps[t]]
            got = jnp.where(tab[6, 2 + t] % 2 == 0, got[0:2], got[2:4])
            triangle = jnp.concatenate(
                [
                    jnp.where(low16, jnp.take_along_axis(pick_row(got, i), unpack, axis=1), 0.0)
                    for i in range(2)
                ],
                axis=0,
            )
            current[t] = mm_exact(triangle, answers[t], TN)[0:16]
        return carry

    lax.fori_loop(0, LAYERS, layer, 0)
    precoders_out[...] = current[...]


def body(channels, precoders_init, receiver_cells, transmitter_cells, interferers, counts):
    dma = pltpu.SemaphoreType.DMA
    vmem = pl.BlockSpec(memory_space=pltpu.VMEM)
    slots = pltpu.VMEM((DEV, 16, 128), F32)
    return pl.pallas_call(
        kernel,
        out_shape=(
            jax.ShapeDtypeStruct((2, 16, 128), F32),
            jax.ShapeDtypeStruct((2, 256), F32),
        ),
        in_specs=[vmem, vmem, vmem, vmem, pl.BlockSpec(memory_space=pl.ANY), vmem],
        out_specs=(vmem, vmem),
        scratch_shapes=[
            pltpu.VMEM((82, 64, 128), F32),
            pltpu.VMEM((82, 128, 128), BF16),
            pltpu.VMEM((2, 16, 128), F32),
            slots, slots, slots, slots, slots,
            pltpu.VMEM((4, 128), F32),
            pltpu.VMEM((DEV, 4, 128), F32),
            pltpu.VMEM((2, 32, 128), BF16),
            pltpu.VMEM((128, 256), F32),
            pltpu.VMEM((128, 256), F32),
            pltpu.VMEM((8, 256), jnp.int32),
            pltpu.SMEM((8, 256), jnp.int32),
            dma, dma, dma, dma((len(GROUPS),)), dma, dma((len(GROUPS),)), dma, dma,
        ],
        compiler_params=pltpu.CompilerParams(collective_id=0, has_side_effects=True),
    )(
        receiver_cells.reshape(1, 256), transmitter_cells.reshape(1, 256), counts.reshape(1, 256), interferers.T,
        channels.reshape(82, 64, 128), precoders_init,
    )


def solution(mesh):
    return jax.shard_map(
        body,
        mesh=mesh,
        in_specs=(P("cells", None, None, None), P("cells", None, None), P(), P(), P(), P()),
        out_specs=(P("cells", None, None), P("cells", None)),
        check_vma=False,
    )
```

time: 192 us -> 180 us (0.938)
  other arithmetic: 5.36 us -> 0 us
  Pallas kernels: 180 us -> 176 us
  local copies, waits for them, and re-layouts: 5.88 us -> 2.55 us
    pallas_call x1, Pallas kernels: 180 us -> 176 us  [body(): pl.pallas_call(kernel, out_shape=(jax.ShapeDtypeStruct((2, 16, 128), F32)...]
where the time goes in v3:
time: 180 us
  Pallas kernels  176 us (98%)
  local copies, waits for them, and re-layouts  2.55 us (1%)
    pallas_call x1, Pallas kernels, body(): pl.pallas_call(kernel, out_shape=(jax.ShapeDtypeStruct((2, 16, 128), F32)...  176 us

profile of v3, /device:TPU:1, one launch (start us, length us, event | category | flops | bytes accessed | tf_op | source)
XLA Modules:
  0.0 179.6 jit_solution(2553103022168193085)
XLA Ops:
  0.6 176.4 %shard_map.77 = (f32[2,16,128]{2,1,0:T(8,128)}, f32[2,256]{1,0:T(2,128)}) custom-call(s32[1,256]{1,0:T(1,128)} %bitcast.7, s32[1,256]{1,0:T(1,128)} %bitcast.8, s32[1,256]{1,0:T(1,128)} %bitcast.9, s32[40,256]{1,0:T(8,128)} %bitcast.6, f32[82,64,128]{2,1,0:T(8,128)} %bitcast.5, f32[2,16,128]{2,1,0:T(8,128)} %first_precoders.1), custom_call_target="tpu_custom_call" | custom-call | tf_op jit(solution)/shard_map/pallas_call | solution.py:365
  177.0 1.3 copy.10
  178.4 1.2 copy.11

commit v4 on v3

--- a/solution.py
+++ b/solution.py
@@ -19,7 +19,6 @@
 SIZES = [8, 8, 16, 16, 16, 16, 16, 16, 8, 8]
 GROUPS = [ORDER[sum(SIZES[:g]) : sum(SIZES[: g + 1])] for g in range(len(SIZES))]
 LAST = len(GROUPS) - 1
-LATE = 7
 NN = (((1,), (0,)), ((), ()))
 NT = (((1,), (1,)), ((), ()))
 TN = (((0,), (0,)), ((), ()))
@@ -161,8 +160,8 @@
 
 def kernel(
     receivers, transmitters, counts, interferers, channels, first_precoders, precoders_out, weights_out,
-    raw, links, current, psend, parr, gbuf, fsend, farr, lsend, larr, pair, acc1, acc2, tabv, tab,
-    raw_sem, tab_sem, psend_sem, precv, fsend_sem, frecv, lsend_sem, lrecv,
+    raw, links, current, psend, parr, gbuf, fsend, farr, lower_rows, pair, acc1, tabv, tab,
+    raw_sem, tab_sem, psend_sem, precv, fsend_sem, frecv,
 ):
     me = lax.axis_index("cells")
     mz, mx, my, mc = me // 32, (me // 8) % 4, (me // 2) % 4, me % 2
@@ -246,12 +245,10 @@
                 highs.append(high)
                 lows.append(low)
             high, low = jnp.concatenate(highs, axis=0), jnp.concatenate(lows, axis=0)
-            one, two = mm(high, high, TN), mm(high, low, TN)
+            one = mm(high, high, TN) + (mm(high, low, TN) + mm(low, high, TN))
             acc1[:, 0:128] = one if g == 0 else acc1[:, 0:128] + one
-            acc2[:, 0:128] = two if g == 0 else acc2[:, 0:128] + two
-
-        cross = acc2[:, 0:128]
-        full = acc1[:, 0:128] + cross + cross.T
+
+        full = acc1[:, 0:128]
         line = lax.broadcasted_iota(jnp.int32, (64, 128), 0)
         spot = lax.broadcasted_iota(jnp.int32, (64, 128), 1) % 64
         covariance = jnp.where(left, full[0:64], full[64:128]) + (line == spot).astype(F32)
@@ -262,7 +259,7 @@
             [jnp.where(half, direct, 0.0), blank, jnp.where(half, 0.0, direct), blank], axis=0
         )
         short = lax.broadcasted_iota(jnp.int32, (16, 128), 0)
-        w = mm_exact(v, apart, NT)
+        w = mm_split(v, apart, NT)
         w = w + (lax.broadcasted_iota(jnp.int32, (16, 128), 1) % 64 == short).astype(F32)
         for s in range(2):
             for i, row in enumerate(pack_rows(w[0:8], w[8:16], s)):
@@ -275,50 +272,57 @@
             pair[s] = jnp.concatenate([high, low], axis=0)
         for s in range(2):
             for i, row in enumerate(pack_rows(lower[0], lower[1], s)):
-                lsend[2 * s + i : 2 * s + i + 1, :] = row
-        larr[0] = lsend[...]
+                lower_rows[s, i : i + 1, :] = row
 
         for g, members in enumerate(GROUPS):
             for k in members:
                 d = 2 * target(k)
                 product = mm(pair[tab[5, d]], links[tab[0, d]], NN)
-                fsend[k] = product[0:16] + product[16:32]
+                fsend[k, 0:16, :] = product[0:16] + product[16:32]
+                fsend[k, 16:18, :] = lower_rows[tab[5, d]]
             for k in members:
                 if k > 0:
                     copy(fsend.at[k], farr.at[k], k, fsend_sem, frecv.at[g]).start()
         farr[0] = fsend[0]
 
         for g, members in enumerate(GROUPS):
-            if g == LATE:
-                for k in ORDER[: DEV - 1]:
-                    copy(lsend, larr.at[k], k, lsend_sem, lrecv).start()
             wait_group(farr, g, fsend_sem, frecv)
             highs, lows, highs01, lows01 = [], [], [], []
             for i in members:
                 d = source(i)
                 m0, m1 = tab[3, 2 * d].astype(F32), tab[4, 2 * d].astype(F32)
-                f = farr[i]
-                highs.append(f.astype(BF16))
+                f = farr[i, 0:16, :]
+                high, low = split(f)
+                highs.append(high)
+                lows.append(low)
                 high, low = split(jnp.concatenate([f * m0, f * m1], axis=1))
                 highs01.append(high)
                 lows01.append(low)
-            high = jnp.concatenate(highs, axis=0)
-            one = mm(high, jnp.concatenate(highs01, axis=0), TN)
-            two = mm(high, jnp.concatenate(lows01, axis=0), TN)
+            high, low = jnp.concatenate(highs, axis=0), jnp.concatenate(lows, axis=0)
+            high01, low01 = jnp.concatenate(highs01, axis=0), jnp.concatenate(lows01, axis=0)
+            one = mm(high, high01, TN) + (mm(high, low01, TN) + mm(low, high01, TN))
             acc1[...] = one if g == 0 else acc1[...] + one
-            acc2[...] = two if g == 0 else acc2[...] + two
 
         mu = jnp.where(index == 0, STEP_SIZES[0], jnp.where(index == 1, STEP_SIZES[1], jnp.where(index == 2, STEP_SIZES[2], STEP_SIZES[3]))).astype(F32)
         eye = (
             lax.broadcasted_iota(jnp.int32, (128, 128), 0) == lax.broadcasted_iota(jnp.int32, (128, 128), 1)
         ).astype(F32) * mu
-        systems = []
+        a0, a1 = acc1[:, 0:128] + eye, acc1[:, 128:256] + eye
+        steps = [slot_from(tab[6, 2 + t] // 2) for t in range(2)]
+        low16 = lanes() < 16
+        unpack = (lanes() + 16 * lax.broadcasted_iota(jnp.int32, (8, 128), 0)) % 128
+        sides = []
         for t in range(2):
-            cross = acc2[:, 128 * t : 128 * t + 128]
-            systems.append(acc1[:, 128 * t : 128 * t + 128] + cross + cross.T + eye)
-        a0, a1 = systems
-        steps = [slot_from(tab[6, 2 + t] // 2) for t in range(2)]
-        b0, b1 = farr[steps[0]], farr[steps[1]]
+            got = farr[steps[t], 16:18, :]
+            triangle = jnp.concatenate(
+                [
+                    jnp.where(low16, jnp.take_along_axis(pick_row(got, i), unpack, axis=1), 0.0)
+                    for i in range(2)
+                ],
+                axis=0,
+            )
+            sides.append(mm_exact(triangle, farr[steps[t], 0:16, :], TN)[0:16])
+        b0, b1 = sides
         upper = jnp.where(left, a0[0:64], a1[64:128])
         under = jnp.where(left, a0[64:128], a1[0:64])
         inverse = invert(rows_of(upper))
@@ -332,63 +336,49 @@
         under = solved[0:64]
         back = jnp.concatenate([jnp.where(left, 0.0, under), jnp.where(left, under, 0.0)], axis=0)
         first = solved[64:80] - mm_split(second, back, NN)
-        answers = [jnp.where(half, first, second), jnp.where(half, second, first)]
-
-        lowers = copy(larr.at[remote], larr.at[remote], ORDER[0], lsend_sem, lrecv)
-        lowers.wait_recv()
-        lowers.wait_send()
         copy(psend.at[remote], parr.at[remote], ORDER[0], psend_sem, precv.at[0]).wait_send()
         copy(fsend.at[remote], farr.at[remote], ORDER[0], fsend_sem, frecv.at[0]).wait_send()
-        low16 = lanes() < 16
-        unpack = (lanes() + 16 * lax.broadcasted_iota(jnp.int32, (8, 128), 0)) % 128
-        for t in range(2):
-            got = larr[steps[t]]
-            got = jnp.where(tab[6, 2 + t] % 2 == 0, got[0:2], got[2:4])
-            triangle = jnp.concatenate(
-                [
-                    jnp.where(low16, jnp.take_along_axis(pick_row(got, i), unpack, axis=1), 0.0)
-                    for i in range(2)
-                ],
-                axis=0,
-            )
-            current[t] = mm_exact(triangle, answers[t], TN)[0:16]
+        current[0] = jnp.where(half, first, second)
+        current[1] = jnp.where(half, second, first)
         return carry
 
     lax.fori_loop(0, LAYERS, layer, 0)
     precoders_out[...] = current[...]
+
+
+def copy_kernel(a_in, b_in, a_out, b_out):
+    a_out[...] = a_in[...]
+    b_out[...] = b_in[...]
 
 
 def body(channels, precoders_init, receiver_cells, transmitter_cells, interferers, counts):
     dma = pltpu.SemaphoreType.DMA
     vmem = pl.BlockSpec(memory_space=pltpu.VMEM)
-    slots = pltpu.VMEM((DEV, 16, 128), F32)
-    return pl.pallas_call(
+    slots, wide = pltpu.VMEM((DEV, 16, 128), F32), pltpu.VMEM((DEV, 18, 128), F32)
+    shapes = (jax.ShapeDtypeStruct((2, 16, 128), F32), jax.ShapeDtypeStruct((2, 256), F32))
+    results = pl.pallas_call(
         kernel,
-        out_shape=(
-            jax.ShapeDtypeStruct((2, 16, 128), F32),
-            jax.ShapeDtypeStruct((2, 256), F32),
-        ),
+        out_shape=shapes,
         in_specs=[vmem, vmem, vmem, vmem, pl.BlockSpec(memory_space=pl.ANY), vmem],
         out_specs=(vmem, vmem),
         scratch_shapes=[
             pltpu.VMEM((82, 64, 128), F32),
             pltpu.VMEM((82, 128, 128), BF16),
             pltpu.VMEM((2, 16, 128), F32),
-            slots, slots, slots, slots, slots,
-            pltpu.VMEM((4, 128), F32),
-            pltpu.VMEM((DEV, 4, 128), F32),
+            slots, slots, slots, wide, wide,
+            pltpu.VMEM((2, 2, 128), F32),
             pltpu.VMEM((2, 32, 128), BF16),
-            pltpu.VMEM((128, 256), F32),
             pltpu.VMEM((128, 256), F32),
             pltpu.VMEM((8, 256), jnp.int32),
             pltpu.SMEM((8, 256), jnp.int32),
-            dma, dma, dma, dma((len(GROUPS),)), dma, dma((len(GROUPS),)), dma, dma,
+            dma, dma, dma, dma((len(GROUPS),)), dma, dma((len(GROUPS),)),
         ],
         compiler_params=pltpu.CompilerParams(collective_id=0, has_side_effects=True),
     )(
         receiver_cells.reshape(1, 256), transmitter_cells.reshape(1, 256), counts.reshape(1, 256), interferers.T,
         channels.reshape(82, 64, 128), precoders_init,
     )
+    return pl.pallas_call(copy_kernel, out_shape=shapes, in_specs=[vmem, vmem], out_specs=(vmem, vmem))(*results)
 
 
 def solution(mesh):

time: 180 us -> 175 us (0.972)
  local copies, waits for them, and re-layouts: 2.55 us -> 0 us
  Pallas kernels: 176 us -> 174 us
    pallas_call x1 -> x2, Pallas kernels: 176 us -> 174 us  [the longest x1 172 us: body(): pl.pallas_call(kernel, out_shape=shapes, in_specs=[vmem, vmem, vmem, vmem...]
    unnamed x2 -> x0, local copies, waits for them, and re-layouts: 2.55 us -> none
where the time goes in v4:
time: 175 us; the launch traced here: 174 us
  Pallas kernels  174 us (99%)
    pallas_call x1, Pallas kernels, body(): pl.pallas_call(kernel, out_shape=shapes, in_specs=[vmem, vmem, vmem, vmem...  172 us

profile of v4, /device:TPU:1, one launch (start us, length us, event | category | flops | bytes accessed | tf_op | source)
XLA Modules:
  0.0 174.4 jit_solution(14441457807347730810)
XLA Ops:
  0.6 172.4 %shard_map.77 = (f32[2,16,128]{2,1,0:T(8,128)}, f32[2,256]{1,0:T(2,128)}) custom-call(s32[1,256]{1,0:T(1,128)} %bitcast.7, s32[1,256]{1,0:T(1,128)} %bitcast.8, s32[1,256]{1,0:T(1,128)} %bitcast.9, s32[40,256]{1,0:T(8,128)} %bitcast.6, f32[82,64,128]{2,1,0:T(8,128)} %bitcast.5, f32[2,16,128]{2,1,0:T(8,128)} %first_precoders.1), custom_call_target="tpu_custom_call" | custom-call | tf_op jit(solution)/shard_map/pallas_call | solution.py:359
  173.0 1.3 shard_map.78

commit v5 on v4

--- a/solution.py
+++ b/solution.py
@@ -16,7 +16,7 @@
 OFFSETS = [(z, x, y, c) for z in range(4) for x in range(4) for y in range(4) for c in range(2)]
 shuffled = random.Random(5)
 ORDER = sorted(range(DEV), key=lambda i: (-sum(min(a, 4 - a) for a in OFFSETS[i][:3]), -i if i < 2 else shuffled.random()))
-SIZES = [8, 8, 16, 16, 16, 16, 16, 16, 8, 8]
+SIZES = [16, 16, 16, 16, 32, 32]
 GROUPS = [ORDER[sum(SIZES[:g]) : sum(SIZES[: g + 1])] for g in range(len(SIZES))]
 LAST = len(GROUPS) - 1
 NN = (((1,), (0,)), ((), ()))

time: 175 us -> 170 us (0.971)
  Pallas kernels: 174 us -> 169 us
    pallas_call x1, Pallas kernels: 172 us -> 168 us  [body(): pl.pallas_call(kernel, out_shape=shapes, in_specs=[vmem, vmem, vmem, vmem...]
where the time goes in v5:
time: 170 us
  Pallas kernels  169 us (99%)
    pallas_call x1, Pallas kernels, body(): pl.pallas_call(kernel, out_shape=shapes, in_specs=[vmem, vmem, vmem, vmem...  168 us

profile of v5, /device:TPU:1, one launch (start us, length us, event | category | flops | bytes accessed | tf_op | source)
XLA Modules:
  0.0 170.0 jit_solution(9870072522180424305)
XLA Ops:
  0.6 168.0 %shard_map.77 = (f32[2,16,128]{2,1,0:T(8,128)}, f32[2,256]{1,0:T(2,128)}) custom-call(s32[1,256]{1,0:T(1,128)} %bitcast.7, s32[1,256]{1,0:T(1,128)} %bitcast.8, s32[1,256]{1,0:T(1,128)} %bitcast.9, s32[40,256]{1,0:T(8,128)} %bitcast.6, f32[82,64,128]{2,1,0:T(8,128)} %bitcast.5, f32[2,16,128]{2,1,0:T(8,128)} %first_precoders.1), custom_call_target="tpu_custom_call" | custom-call | tf_op jit(solution)/shard_map/pallas_call | solution.py:359
  168.7 1.3 shard_map.78

commit v6 on v5

--- a/solution.py
+++ b/solution.py
@@ -261,9 +261,6 @@
         short = lax.broadcasted_iota(jnp.int32, (16, 128), 0)
         w = mm_split(v, apart, NT)
         w = w + (lax.broadcasted_iota(jnp.int32, (16, 128), 1) % 64 == short).astype(F32)
-        for s in range(2):
-            for i, row in enumerate(pack_rows(w[0:8], w[8:16], s)):
-                weights_out[s : s + 1, 128 * i : 128 * i + 128] = row
         lower, filters = lower_divide(w, v)
         for s in range(2):
             mine = jnp.where(half, filters, 0.0) if s == 0 else jnp.where(half, 0.0, filters)
@@ -275,15 +272,20 @@
                 lower_rows[s, i : i + 1, :] = row
 
         for g, members in enumerate(GROUPS):
-            for k in members:
-                d = 2 * target(k)
-                product = mm(pair[tab[5, d]], links[tab[0, d]], NN)
-                fsend[k, 0:16, :] = product[0:16] + product[16:32]
-                fsend[k, 16:18, :] = lower_rows[tab[5, d]]
-            for k in members:
-                if k > 0:
-                    copy(fsend.at[k], farr.at[k], k, fsend_sem, frecv.at[g]).start()
+            width = 8 if g == 0 else 16
+            for batch in [members[i : i + width] for i in range(0, len(members), width)]:
+                for k in batch:
+                    d = 2 * target(k)
+                    product = mm(pair[tab[5, d]], links[tab[0, d]], NN)
+                    fsend[k, 0:16, :] = product[0:16] + product[16:32]
+                    fsend[k, 16:18, :] = lower_rows[tab[5, d]]
+                for k in batch:
+                    if k > 0:
+                        copy(fsend.at[k], farr.at[k], k, fsend_sem, frecv.at[g]).start()
         farr[0] = fsend[0]
+        for s in range(2):
+            for i, row in enumerate(pack_rows(w[0:8], w[8:16], s)):
+                weights_out[s : s + 1, 128 * i : 128 * i + 128] = row
 
         for g, members in enumerate(GROUPS):
             wait_group(farr, g, fsend_sem, frecv)

time: 170 us -> 171 us (level)
  no operation moved by 1% of the time
where the time goes in v6:
time: 171 us; the launch traced here: 170 us
  Pallas kernels  170 us (99%)
    pallas_call x1, Pallas kernels, body(): pl.pallas_call(kernel, out_shape=shapes, in_specs=[vmem, vmem, vmem, vmem...  168 us

profile of v6, /device:TPU:1, one launch (start us, length us, event | category | flops | bytes accessed | tf_op | source)
XLA Modules:
  0.0 170.5 jit_solution(1327171813225301453)
XLA Ops:
  0.6 168.5 %shard_map.77 = (f32[2,16,128]{2,1,0:T(8,128)}, f32[2,256]{1,0:T(2,128)}) custom-call(s32[1,256]{1,0:T(1,128)} %bitcast.7, s32[1,256]{1,0:T(1,128)} %bitcast.8, s32[1,256]{1,0:T(1,128)} %bitcast.9, s32[40,256]{1,0:T(8,128)} %bitcast.6, f32[82,64,128]{2,1,0:T(8,128)} %bitcast.5, f32[2,16,128]{2,1,0:T(8,128)} %first_precoders.1), custom_call_target="tpu_custom_call" | custom-call | tf_op jit(solution)/shard_map/pallas_call | solution.py:361
  169.1 1.3 shard_map.78
